TPU v7x, 128 devices: a whole 4x4x4 slice. The times are simulated.
128 devices in a mesh: rows: 32 (over x_lo, y, z), offs: 4 (over x_hi, core).
Axes of the slice: x: 4 (x_hi: 2, x_lo: 2; x = x_hi * 2 + x_lo), y: 4, z: 4, core: 2. Of those that a mesh axis runs over, the one named last changes fastest.
Arguments:
- coherency_field: float32 [9, 2048, 1024], P(None, 'rows', 'offs'), may hold values from -2 to 5, as said below
- offsets: int32 [120, 2], replicated, may hold values from -6 to 6, as said below
Outputs:
- despeckled: float32 [9, 2048, 1024], P(None, 'rows', 'offs')
Inputs may be any that keep to these rules, and one draw needn't show every extreme that they name: `coherency_field`: each pixel's channels form a positive definite Hermitian matrix in the layout of the steps. The offsets are distinct, none is (0, 0), and both components of each lie in -6..6.
All inputs are finite; a program needn't handle non-finite values.
Results may differ from a plain program's by a relative error of at most 0.0001.
Values sent between devices are 32-bit elements; how exact they have to be, the bound alone decides.
A program may use at most 64 MiB of HBM per device.

v0:
```python
import jax
import jax.numpy as jnp
from jax import lax
from jax.sharding import PartitionSpec as P

SEARCH = 6
PATCH = 3


filter_strength = 1.5


def with_halo(cells, sides, width):
    for axis, dim in sides:
        count = lax.axis_size(axis)
        ends = count - 1
        head = lax.slice_in_dim(cells, 0, width, axis=dim)
        tail = lax.slice_in_dim(cells, cells.shape[dim] - width, cells.shape[dim], axis=dim)
        cells = jnp.concatenate(
            [
                lax.ppermute(tail, axis, [(i, (i + 1) % count) for i in range(ends)]),
                cells,
                lax.ppermute(head, axis, [((i + 1) % count, i) for i in range(ends)]),
            ],
            axis=dim,
        )
    return cells


def hermitian_inverse(matrix):
    diag_one, diag_two, diag_three = (matrix[0], matrix[1], matrix[2])
    re_onetwo, re_onethree, re_twothree = (matrix[3], matrix[4], matrix[5])
    im_onetwo, im_onethree, im_twothree = (matrix[6], matrix[7], matrix[8])
    abs_onetwo = re_onetwo * re_onetwo + im_onetwo * im_onetwo
    abs_onethree = re_onethree * re_onethree + im_onethree * im_onethree
    abs_twothree = re_twothree * re_twothree + im_twothree * im_twothree
    yz_real = re_onethree * re_twothree + im_onethree * im_twothree
    yz_imag = im_onethree * re_twothree - re_onethree * im_twothree
    xz_real = re_onetwo * re_twothree - im_onetwo * im_twothree
    xz_imag = re_onetwo * im_twothree + im_onetwo * re_twothree
    yx_real = re_onethree * re_onetwo + im_onethree * im_onetwo
    yx_imag = im_onethree * re_onetwo - re_onethree * im_onetwo
    triple_real = xz_real * re_onethree + xz_imag * im_onethree
    determinant = (
        diag_one * diag_two * diag_three
        + 2.0 * triple_real
        - diag_one * abs_twothree
        - diag_two * abs_onethree
        - diag_three * abs_onetwo
    )
    adjugate = jnp.stack(
        [
            diag_two * diag_three - abs_twothree,
            diag_one * diag_three - abs_onethree,
            diag_one * diag_two - abs_onetwo,
            -(re_onetwo * diag_three - yz_real),
            xz_real - re_onethree * diag_two,
            -(diag_one * re_twothree - yx_real),
            -(im_onetwo * diag_three - yz_imag),
            xz_imag - im_onethree * diag_two,
            -(diag_one * im_twothree - yx_imag),
        ],
        0,
    )
    return adjugate / determinant[None]


def pair_trace(left, right):
    return jnp.sum(left[:3] * right[:3], 0) + 2.0 * jnp.sum(left[3:] * right[3:], 0)


def window_sum(values, row_count, col_count):
    side = 2 * PATCH + 1
    partial_rows = values[0:row_count]
    for shift in range(1, side):
        partial_rows = partial_rows + values[shift : shift + row_count]
    total = partial_rows[:, 0:col_count]
    for shift in range(1, side):
        total = total + partial_rows[:, shift : shift + col_count]
    return total


def accumulate(coherency, inverse, validity, offset_list, row_count, col_count):
    span_rows = row_count + 2 * PATCH
    span_cols = col_count + 2 * PATCH
    own_cov = coherency[:, SEARCH : SEARCH + span_rows, SEARCH : SEARCH + span_cols]
    own_inv = inverse[:, SEARCH : SEARCH + span_rows, SEARCH : SEARCH + span_cols]
    own_valid = validity[SEARCH : SEARCH + span_rows, SEARCH : SEARCH + span_cols]
    chans = coherency.shape[0]

    def advance(turn, totals):
        numerator, denominator = totals
        top = SEARCH + offset_list[turn, 0]
        left = SEARCH + offset_list[turn, 1]
        anchor = jnp.zeros((), jnp.int32)
        other_cov = lax.dynamic_slice(coherency, (anchor, top, left), (chans, span_rows, span_cols))
        other_inv = lax.dynamic_slice(inverse, (anchor, top, left), (chans, span_rows, span_cols))
        other_valid = lax.dynamic_slice(validity, (top, left), (span_rows, span_cols))
        distance = (pair_trace(own_inv, other_cov) + pair_trace(own_cov, other_inv) - 6.0) * (
            own_valid * other_valid
        )
        patch = window_sum(distance, row_count, col_count) / float((2 * PATCH + 1) ** 2)
        weight = (
            jnp.exp(-patch / filter_strength)
            * other_valid[PATCH : PATCH + row_count, PATCH : PATCH + col_count]
        )
        numerator = (
            numerator
            + weight[None] * other_cov[:, PATCH : PATCH + row_count, PATCH : PATCH + col_count]
        )
        denominator = denominator + weight
        return (numerator, denominator)

    start = (
        jnp.zeros((chans, row_count, col_count), jnp.float32),
        jnp.zeros((row_count, col_count), jnp.float32),
    )
    return lax.fori_loop(0, offset_list.shape[0], advance, start)


def strip_validity(first_row, first_col, row_span, col_span, row_total, col_total):
    row_ids = first_row + jnp.arange(row_span, dtype=jnp.int32)
    col_ids = first_col + jnp.arange(col_span, dtype=jnp.int32)
    inside_rows = (row_ids >= 0) & (row_ids < row_total)
    inside_cols = (col_ids >= 0) & (col_ids < col_total)
    return (inside_rows[:, None] & inside_cols[None, :]).astype(jnp.float32)


def per_device(coherency_field, offsets):
    chans, row_count, col_count = coherency_field.shape
    rim = SEARCH + PATCH
    row_total = row_count * lax.axis_size("rows")
    col_total = col_count * lax.axis_size("offs")
    row_start = lax.axis_index("rows") * row_count
    payload = jnp.concatenate([coherency_field, hermitian_inverse(coherency_field)], 0)
    wide = lax.all_gather(payload, "offs", axis=2, tiled=True)
    padded = with_halo(wide, (("rows", 1),), rim)
    padded = jnp.pad(padded, ((0, 0), (0, 0), (rim, rim)))
    first_col = jnp.zeros((), jnp.int32)
    own_count = offsets.shape[0] // lax.axis_size("offs")
    own_offsets = lax.dynamic_slice_in_dim(
        offsets, lax.axis_index("offs") * own_count, own_count, 0
    )
    validity = strip_validity(
        row_start - rim,
        first_col - rim,
        row_count + 2 * rim,
        col_total + 2 * rim,
        row_total,
        col_total,
    )
    coherency = padded[:chans]
    inverse = jnp.where(validity[None] > 0, padded[chans:], 0.0)
    numerator, denominator = accumulate(
        coherency, inverse, validity, own_offsets, row_count, col_total
    )
    numerator, denominator = (
        lax.psum_scatter(numerator, "offs", scatter_dimension=2, tiled=True),
        lax.psum_scatter(denominator[None], "offs", scatter_dimension=2, tiled=True),
    )
    denominator = denominator[0]
    return (coherency_field + numerator) / (1.0 + denominator)[None]


def solution(mesh):
    in_specs = (P(None, "rows", "offs"), P())
    out_specs = P(None, "rows", "offs")
    return jax.shard_map(
        per_device, mesh=mesh, in_specs=in_specs, out_specs=out_specs, check_vma=False
    )
```

profile of v0, /device:TPU:1, one launch (start us, length us, event | category | flops | bytes accessed | tf_op | source)
XLA Modules:
  0.0 709.7 jit_solution(5958215094824503350)
XLA Ops:
  15.1 45.2 %all-gather.2.cloned.1.call-done = f32[18,64,1024]{2,1,0:T(8,128)} async-done(((f32[18,64,256]{2,1,0:T(8,128)}), f32[18,64,1024]{2,1,0:T(8,128)}) %all-gather.2.cloned.1.call-update) | async-done | bytes 4718608 | tf_op jit(solution)/shard_map/all_gather | solution.py:136
  69.5 16.2 %collective-permute-done = f32[18,9,1024]{2,0,1:T(8,128)S(1)} collective-permute-done((f32[18,9,1024]{2,0,1:T(8,128)}, f32[18,9,1024]{2,0,1:T(8,128)S(1)}, u32[]{:S(2)}, u32[]{:S(2)}) %collective-permute-start) | collective-permute-done | bytes 663584 | tf_op jit(solution)/shard_map/ppermute | solution.py:21
  91.3 5.3 select_maximum_fusion
  102.9 525.4 %while.18 = (s32[]{:T(128)}, f32[9,64,1024]{2,1,0:T(8,128)}, f32[64,1024]{1,0:T(8,128)}, f32[9,70,1030]{2,1,0:T(8,128)}, s32[30,2]{0,1:T(2,128)S(1)}, /*index=5*...) while((s32[]{:T(128)}, f32[9,64,1024]{2,1,0:T(8,128)}, ...), condition=%wide.region_5.6_spmd.clone, body=%wide.region_0.5_spmd.clone.sunk | while | flops 5835438 | bytes 29776096 | solution.py:118
  106.2 4.1 fusion.19
  123.0 4.1 fusion.19
  132.4 4.8 fusion.20
  140.5 4.1 fusion.19
  150.0 4.8 fusion.20
  158.0 4.1 fusion.19
  167.5 4.8 fusion.20
  185.0 4.8 fusion.20
  193.1 4.1 fusion.19
  202.6 4.8 fusion.20
  220.1 4.8 fusion.20
  237.7 4.8 fusion.20
  245.7 4.1 fusion.19
  255.2 4.8 fusion.20
  263.3 4.1 fusion.19
  272.7 4.8 fusion.20
  280.8 4.1 fusion.19
  290.3 4.8 fusion.20
  307.8 4.8 fusion.20
  325.4 4.8 fusion.20
  342.9 4.8 fusion.20
  360.4 4.8 fusion.20
  378.0 4.8 fusion.20
  395.5 4.8 fusion.20
  403.6 4.1 fusion.19
  413.1 4.8 fusion.20
  421.1 4.1 fusion.19
  430.6 4.8 fusion.20
  438.7 4.1 fusion.19
  448.2 4.8 fusion.20
  465.7 4.8 fusion.20
  473.8 4.1 fusion.19
  483.2 4.8 fusion.20
  500.8 4.8 fusion.20
  518.3 4.8 fusion.20
  535.9 4.8 fusion.20
  553.4 4.8 fusion.20
  570.9 4.8 fusion.20
  588.5 4.8 fusion.20
  596.6 4.1 fusion.19
  606.0 4.8 fusion.20
  623.6 4.8 fusion.20
  629.1 29.7 %reduce-scatter.5.cloned.1.call-done = f32[1,64,256]{2,1,0:T(8,128)} async-done(((f32[1,64,1024]{2,1,0:T(8,128)}), f32[1,64,256]{2,1,0:T(8,128)}) %reduce-scatter.5.cloned.1.call-update) | async-done | bytes 65552 | tf_op jit(solution)/shard_map/reduce_scatter | solution.py:159
  659.7 41.5 %reduce-scatter.3.cloned.1.call-done = f32[9,64,256]{2,1,0:T(8,128)} async-done(((f32[9,64,1024]{2,1,0:T(8,128)}), f32[9,64,256]{2,1,0:T(8,128)}) %reduce-scatter.3.cloned.1.call-update) | async-done | bytes 589840 | tf_op jit(solution)/shard_map/reduce_scatter | solution.py:158
  (393 shorter events, 287.3 us)
Async XLA Ops:
  6.5 62.9 %copy-start = (s32[120,2]{0,1:T(2,128)S(1)}, s32[120,2]{0,1:T(2,128)}, u32[]{:S(2)}) copy-start(s32[120,2]{0,1:T(2,128)} %param.5) | copy-start | bytes 2884
  6.5 7.1 %copy-start.4 = (f32[9,64,256]{2,1,0:T(8,128)S(1)}, f32[9,64,256]{2,1,0:T(8,128)}, u32[]{:S(2)}) copy-start(f32[9,64,256]{2,1,0:T(8,128)} %param.4) | copy-start | bytes 1769476
  6.5 53.7 %all-gather.2.cloned.1.call-start = ((), (), s32[]{:S(2)}) async-start(), calls=%async_computation.2 | async-start | bytes 5898240 | tf_op jit(solution)/shard_map/all_gather | solution.py:136
  15.0 643.8 %reduce-scatter.5.cloned.1.call-start = ((), (), s32[]{:S(2)}) async-start(), calls=%async_computation.4 | async-start | bytes 327680 | tf_op jit(solution)/shard_map/reduce_scatter | solution.py:159
  63.5 22.3 %collective-permute-start = (f32[18,9,1024]{2,0,1:T(8,128)}, f32[18,9,1024]{2,0,1:T(8,128)S(1)}, u32[]{:S(2)}, u32[]{:S(2)}) collective-permute-start(f32[18,9,1024]{2,0,1:T(8,128)} %copy.17), channel_id=1, source_target_pairs={{0,4},{4,8},{8,12},{12,16},{16,20},{20,24},{24,28},{28,32},{32,36}... | collective-permute-start | bytes 1990664 | tf_op jit(solution)/shard_map/ppermute | solution.py:21
  67.1 22.7 %collective-permute-start.1 = (f32[18,9,1024]{2,0,1:T(8,128)S(1)}, f32[18,9,1024]{2,0,1:T(8,128)}, u32[]{:S(2)}, u32[]{:S(2)}) collective-permute-start(f32[18,9,1024]{2,0,1:T(8,128)S(1)} %copy.18), channel_id=1, source_target_pairs={{4,0},{8,4},{12,8},{16,12},{20,16},{24,20},{28,24},{32,28},{36,32}... | collective-permute-start | bytes 1990664 | tf_op jit(solution)/shard_map/ppermute | solution.py:23
  102.9 10.0 %copy-start.2 = (f32[82,1042]{1,0:T(8,128)}, f32[82,1042]{1,0:T(8,128)S(1)}, u32[]{:S(2)}) copy-start(f32[82,1042]{1,0:T(8,128)S(1)} %get-tuple-element.450) | copy-start | bytes 1025332 | tf_op jit(solution)/shard_map/while
  119.6 10.0 %copy-start.2 = (f32[82,1042]{1,0:T(8,128)}, f32[82,1042]{1,0:T(8,128)S(1)}, u32[]{:S(2)}) copy-start(f32[82,1042]{1,0:T(8,128)S(1)} %get-tuple-element.450) | copy-start | bytes 1025332 | tf_op jit(solution)/shard_map/while
  137.2 10.0 %copy-start.2 = (f32[82,1042]{1,0:T(8,128)}, f32[82,1042]{1,0:T(8,128)S(1)}, u32[]{:S(2)}) copy-start(f32[82,1042]{1,0:T(8,128)S(1)} %get-tuple-element.450) | copy-start | bytes 1025332 | tf_op jit(solution)/shard_map/while
  150.0 4.8 copy-start.3
  154.7 10.0 %copy-start.2 = (f32[82,1042]{1,0:T(8,128)}, f32[82,1042]{1,0:T(8,128)S(1)}, u32[]{:S(2)}) copy-start(f32[82,1042]{1,0:T(8,128)S(1)} %get-tuple-element.450) | copy-start | bytes 1025332 | tf_op jit(solution)/shard_map/while
  167.5 4.8 copy-start.3
  172.3 10.0 %copy-start.2 = (f32[82,1042]{1,0:T(8,128)}, f32[82,1042]{1,0:T(8,128)S(1)}, u32[]{:S(2)}) copy-start(f32[82,1042]{1,0:T(8,128)S(1)} %get-tuple-element.450) | copy-start | bytes 1025332 | tf_op jit(solution)/shard_map/while
  185.0 4.8 copy-start.3
  189.8 10.0 %copy-start.2 = (f32[82,1042]{1,0:T(8,128)}, f32[82,1042]{1,0:T(8,128)S(1)}, u32[]{:S(2)}) copy-start(f32[82,1042]{1,0:T(8,128)S(1)} %get-tuple-element.450) | copy-start | bytes 1025332 | tf_op jit(solution)/shard_map/while
  202.6 4.8 copy-start.3
  207.3 10.0 %copy-start.2 = (f32[82,1042]{1,0:T(8,128)}, f32[82,1042]{1,0:T(8,128)S(1)}, u32[]{:S(2)}) copy-start(f32[82,1042]{1,0:T(8,128)S(1)} %get-tuple-element.450) | copy-start | bytes 1025332 | tf_op jit(solution)/shard_map/while
  224.9 10.0 %copy-start.2 = (f32[82,1042]{1,0:T(8,128)}, f32[82,1042]{1,0:T(8,128)S(1)}, u32[]{:S(2)}) copy-start(f32[82,1042]{1,0:T(8,128)S(1)} %get-tuple-element.450) | copy-start | bytes 1025332 | tf_op jit(solution)/shard_map/while
  237.7 4.8 copy-start.3
  242.4 10.0 %copy-start.2 = (f32[82,1042]{1,0:T(8,128)}, f32[82,1042]{1,0:T(8,128)S(1)}, u32[]{:S(2)}) copy-start(f32[82,1042]{1,0:T(8,128)S(1)} %get-tuple-element.450) | copy-start | bytes 1025332 | tf_op jit(solution)/shard_map/while
  255.2 4.8 copy-start.3
  260.0 10.0 %copy-start.2 = (f32[82,1042]{1,0:T(8,128)}, f32[82,1042]{1,0:T(8,128)S(1)}, u32[]{:S(2)}) copy-start(f32[82,1042]{1,0:T(8,128)S(1)} %get-tuple-element.450) | copy-start | bytes 1025332 | tf_op jit(solution)/shard_map/while
  272.7 4.8 copy-start.3
  277.5 10.0 %copy-start.2 = (f32[82,1042]{1,0:T(8,128)}, f32[82,1042]{1,0:T(8,128)S(1)}, u32[]{:S(2)}) copy-start(f32[82,1042]{1,0:T(8,128)S(1)} %get-tuple-element.450) | copy-start | bytes 1025332 | tf_op jit(solution)/shard_map/while
  290.3 4.8 copy-start.3
  295.0 10.0 %copy-start.2 = (f32[82,1042]{1,0:T(8,128)}, f32[82,1042]{1,0:T(8,128)S(1)}, u32[]{:S(2)}) copy-start(f32[82,1042]{1,0:T(8,128)S(1)} %get-tuple-element.450) | copy-start | bytes 1025332 | tf_op jit(solution)/shard_map/while
  307.8 4.8 copy-start.3
  312.6 10.0 %copy-start.2 = (f32[82,1042]{1,0:T(8,128)}, f32[82,1042]{1,0:T(8,128)S(1)}, u32[]{:S(2)}) copy-start(f32[82,1042]{1,0:T(8,128)S(1)} %get-tuple-element.450) | copy-start | bytes 1025332 | tf_op jit(solution)/shard_map/while
  325.4 4.8 copy-start.3
  330.1 10.0 %copy-start.2 = (f32[82,1042]{1,0:T(8,128)}, f32[82,1042]{1,0:T(8,128)S(1)}, u32[]{:S(2)}) copy-start(f32[82,1042]{1,0:T(8,128)S(1)} %get-tuple-element.450) | copy-start | bytes 1025332 | tf_op jit(solution)/shard_map/while
  347.7 10.0 %copy-start.2 = (f32[82,1042]{1,0:T(8,128)}, f32[82,1042]{1,0:T(8,128)S(1)}, u32[]{:S(2)}) copy-start(f32[82,1042]{1,0:T(8,128)S(1)} %get-tuple-element.450) | copy-start | bytes 1025332 | tf_op jit(solution)/shard_map/while
  365.2 10.0 %copy-start.2 = (f32[82,1042]{1,0:T(8,128)}, f32[82,1042]{1,0:T(8,128)S(1)}, u32[]{:S(2)}) copy-start(f32[82,1042]{1,0:T(8,128)S(1)} %get-tuple-element.450) | copy-start | bytes 1025332 | tf_op jit(solution)/shard_map/while
  382.8 10.0 %copy-start.2 = (f32[82,1042]{1,0:T(8,128)}, f32[82,1042]{1,0:T(8,128)S(1)}, u32[]{:S(2)}) copy-start(f32[82,1042]{1,0:T(8,128)S(1)} %get-tuple-element.450) | copy-start | bytes 1025332 | tf_op jit(solution)/shard_map/while
  400.3 10.0 %copy-start.2 = (f32[82,1042]{1,0:T(8,128)}, f32[82,1042]{1,0:T(8,128)S(1)}, u32[]{:S(2)}) copy-start(f32[82,1042]{1,0:T(8,128)S(1)} %get-tuple-element.450) | copy-start | bytes 1025332 | tf_op jit(solution)/shard_map/while
  417.8 10.0 %copy-start.2 = (f32[82,1042]{1,0:T(8,128)}, f32[82,1042]{1,0:T(8,128)S(1)}, u32[]{:S(2)}) copy-start(f32[82,1042]{1,0:T(8,128)S(1)} %get-tuple-element.450) | copy-start | bytes 1025332 | tf_op jit(solution)/shard_map/while
  435.4 10.0 %copy-start.2 = (f32[82,1042]{1,0:T(8,128)}, f32[82,1042]{1,0:T(8,128)S(1)}, u32[]{:S(2)}) copy-start(f32[82,1042]{1,0:T(8,128)S(1)} %get-tuple-element.450) | copy-start | bytes 1025332 | tf_op jit(solution)/shard_map/while
  452.9 10.0 %copy-start.2 = (f32[82,1042]{1,0:T(8,128)}, f32[82,1042]{1,0:T(8,128)S(1)}, u32[]{:S(2)}) copy-start(f32[82,1042]{1,0:T(8,128)S(1)} %get-tuple-element.450) | copy-start | bytes 1025332 | tf_op jit(solution)/shard_map/while
  470.5 10.0 %copy-start.2 = (f32[82,1042]{1,0:T(8,128)}, f32[82,1042]{1,0:T(8,128)S(1)}, u32[]{:S(2)}) copy-start(f32[82,1042]{1,0:T(8,128)S(1)} %get-tuple-element.450) | copy-start | bytes 1025332 | tf_op jit(solution)/shard_map/while
  488.0 10.0 %copy-start.2 = (f32[82,1042]{1,0:T(8,128)}, f32[82,1042]{1,0:T(8,128)S(1)}, u32[]{:S(2)}) copy-start(f32[82,1042]{1,0:T(8,128)S(1)} %get-tuple-element.450) | copy-start | bytes 1025332 | tf_op jit(solution)/shard_map/while
  505.5 10.0 %copy-start.2 = (f32[82,1042]{1,0:T(8,128)}, f32[82,1042]{1,0:T(8,128)S(1)}, u32[]{:S(2)}) copy-start(f32[82,1042]{1,0:T(8,128)S(1)} %get-tuple-element.450) | copy-start | bytes 1025332 | tf_op jit(solution)/shard_map/while
  523.1 10.0 %copy-start.2 = (f32[82,1042]{1,0:T(8,128)}, f32[82,1042]{1,0:T(8,128)S(1)}, u32[]{:S(2)}) copy-start(f32[82,1042]{1,0:T(8,128)S(1)} %get-tuple-element.450) | copy-start | bytes 1025332 | tf_op jit(solution)/shard_map/while
  540.6 10.0 %copy-start.2 = (f32[82,1042]{1,0:T(8,128)}, f32[82,1042]{1,0:T(8,128)S(1)}, u32[]{:S(2)}) copy-start(f32[82,1042]{1,0:T(8,128)S(1)} %get-tuple-element.450) | copy-start | bytes 1025332 | tf_op jit(solution)/shard_map/while
  558.2 10.0 %copy-start.2 = (f32[82,1042]{1,0:T(8,128)}, f32[82,1042]{1,0:T(8,128)S(1)}, u32[]{:S(2)}) copy-start(f32[82,1042]{1,0:T(8,128)S(1)} %get-tuple-element.450) | copy-start | bytes 1025332 | tf_op jit(solution)/shard_map/while
  575.7 10.0 %copy-start.2 = (f32[82,1042]{1,0:T(8,128)}, f32[82,1042]{1,0:T(8,128)S(1)}, u32[]{:S(2)}) copy-start(f32[82,1042]{1,0:T(8,128)S(1)} %get-tuple-element.450) | copy-start | bytes 1025332 | tf_op jit(solution)/shard_map/while
  593.2 10.0 %copy-start.2 = (f32[82,1042]{1,0:T(8,128)}, f32[82,1042]{1,0:T(8,128)S(1)}, u32[]{:S(2)}) copy-start(f32[82,1042]{1,0:T(8,128)S(1)} %get-tuple-element.450) | copy-start | bytes 1025332 | tf_op jit(solution)/shard_map/while
  610.8 10.0 %copy-start.2 = (f32[82,1042]{1,0:T(8,128)}, f32[82,1042]{1,0:T(8,128)S(1)}, u32[]{:S(2)}) copy-start(f32[82,1042]{1,0:T(8,128)S(1)} %get-tuple-element.450) | copy-start | bytes 1025332 | tf_op jit(solution)/shard_map/while
  628.3 72.8 %copy-start.5 = (f32[9,64,256]{2,1,0:T(8,128)S(1)}, f32[9,64,256]{2,1,0:T(8,128)}, u32[]{:S(2)}) copy-start(f32[9,64,256]{2,1,0:T(8,128)} %param.4) | copy-start | bytes 1769476
  628.4 72.8 %reduce-scatter.3.cloned.1.call-start = ((), (), s32[]{:S(2)}) async-start(), calls=%async_computation.3 | async-start | bytes 2949120 | tf_op jit(solution)/shard_map/reduce_scatter | solution.py:158
  (51 other events, 175.1 us)
Sparse Core Ops, SparseCore 0:
  15.1 45.0 all-gather.1
  628.5 30.3 reduce-scatter.4
  661.7 39.4 reduce-scatter.2
where the time goes:
time: 712 us; the launch traced here: 710 us
  other arithmetic  443 us (62%)
  waiting for transfers between devices  137 us (19%)
  loops' own time  79.6 us (11%)
  local copies, waits for them, and re-layouts  32.2 us (5%)
  between operations  13.3 us (2%)
    add x30, other arithmetic, advance(): numerator + weight[None] * other_cov[:, PATCH:PATCH + row_count, PATCH:PA...  142 us
    reduce_sum x30, other arithmetic, pair_trace(): jnp.sum(left[3:] * right[3:], 0)  124 us
    another operation x1, loops' own time, accumulate(): return lax.fori_loop(0, offset_list.shape[0], advance, start)  79.6 us
    reduce_sum x30, other arithmetic, pair_trace(): jnp.sum(left[:3] * right[:3], 0) + 2.0 * jnp.sum(left[3:] * right[3:], 0)  76.9 us
    add x30, other arithmetic, advance(): denominator = denominator + weight  70.1 us
    all_gather x1, waiting for transfers between devices, per_device(): wide = lax.all_gather(payload, 'offs', axis=2, tiled=True)  45.2 us
    reduce_scatter x1, waiting for transfers between devices, per_device(): lax.psum_scatter(numerator, 'offs', scatter_dimension=2, tiled=True)  41.5 us
    reduce_scatter x1, waiting for transfers between devices, per_device(): lax.psum_scatter(denominator[None], 'offs', scatter_dimension=2, tiled=True)  29.7 us
  transfers between devices with their start and end apart: 5, of which 5 were waited for; matrix products, arithmetic and copies ran while one was open for 0% of the time, Pallas kernels for 0%

commit v1 on v0

v1 whole, which is shorter than its diff:
```python
import functools
import math

import jax
import jax.numpy as jnp
import numpy as np
from jax import lax
from jax.experimental import pallas as pl
from jax.experimental.pallas import tpu as pltpu
from jax.sharding import PartitionSpec as P

SEARCH = 6
PATCH = 3
SIDE = 2 * PATCH + 1
SPAN = 2 * SEARCH + 1
RIM = SEARCH + PATCH
STRENGTH = 1.5
LANES = 128
PAD = 16
CHANS = 9
FEATS = 2 * CHANS + 1
BATCH = 8
EXPONENT = -math.log2(math.e) / (STRENGTH * SIDE * SIDE)


def hermitian_inverse(matrix):
    diag_one, diag_two, diag_three = matrix[0], matrix[1], matrix[2]
    re_onetwo, re_onethree, re_twothree = matrix[3], matrix[4], matrix[5]
    im_onetwo, im_onethree, im_twothree = matrix[6], matrix[7], matrix[8]
    abs_onetwo = re_onetwo * re_onetwo + im_onetwo * im_onetwo
    abs_onethree = re_onethree * re_onethree + im_onethree * im_onethree
    abs_twothree = re_twothree * re_twothree + im_twothree * im_twothree
    yz_real = re_onethree * re_twothree + im_onethree * im_twothree
    yz_imag = im_onethree * re_twothree - re_onethree * im_twothree
    xz_real = re_onetwo * re_twothree - im_onetwo * im_twothree
    xz_imag = re_onetwo * im_twothree + im_onetwo * re_twothree
    yx_real = re_onethree * re_onetwo + im_onethree * im_onetwo
    yx_imag = im_onethree * re_onetwo - re_onethree * im_onetwo
    triple_real = xz_real * re_onethree + xz_imag * im_onethree
    determinant = (
        diag_one * diag_two * diag_three
        + 2.0 * triple_real
        - diag_one * abs_twothree
        - diag_two * abs_onethree
        - diag_three * abs_onetwo
    )
    adjugate = [
        diag_two * diag_three - abs_twothree,
        diag_one * diag_three - abs_onethree,
        diag_one * diag_two - abs_onetwo,
        -(re_onetwo * diag_three - yz_real),
        xz_real - re_onethree * diag_two,
        -(diag_one * re_twothree - yx_real),
        -(im_onetwo * diag_three - yz_imag),
        xz_imag - im_onethree * diag_two,
        -(diag_one * im_twothree - yx_imag),
    ]
    return adjugate, determinant


def band_matrix(cols):
    source = np.arange(cols)[:, None]
    target = np.arange(cols)[None, :]
    main = (np.abs(source - target) <= PATCH).astype(np.float32)
    edge = np.zeros((LANES, cols), np.float32)
    for turn in range(SPAN):
        for place in range(2 * PATCH):
            column = place - PATCH if place < PATCH else cols + place - PATCH
            edge[8 * turn + place] = np.abs(np.arange(cols) - column) <= PATCH
    return np.concatenate([main, main, edge, edge], 0)


def select_matrix():
    pick = np.zeros((LANES, 2 * LANES), np.float32)
    for turn in range(SPAN):
        for place in range(2 * PATCH):
            lane = 32 + place - PATCH if place < PATCH else 96 + place - PATCH
            pick[lane, 8 * turn + place] = 1.0
            pick[lane + turn - SEARCH, LANES + 8 * turn + place] = 1.0
    return pick


def gain(feature):
    if feature == 2 * CHANS:
        return -6.0
    return 1.0 if feature % CHANS < 3 else 2.0


def partner(feature):
    if feature == 2 * CHANS:
        return feature
    return (feature + CHANS) % (2 * CHANS)


def despeckle(
    sizes, offs_ref, origin_ref, main_ref, left_ref, right_ref, band_ref, pick_ref, out_ref,
    feats, moved, own, edges, edge_own, edge_other, edge_dist, edge_sum, dist, sums, weights, totals,
):
    rows, cols, row_total, col_total = sizes
    span_rows = rows + 2 * PAD
    row_tiles = span_rows // 8
    halves = cols // LANES
    dist_rows = rows + 8
    lane = lax.broadcasted_iota(jnp.int32, (8, LANES), 1)
    sub = lax.broadcasted_iota(jnp.int32, (8, LANES), 0)
    row_start, col_start = origin_ref[0], origin_ref[1]
    f32, bf16 = jnp.float32, jnp.bfloat16

    def features(tile, _):
        at = pl.ds(pl.multiple_of(tile * 8, 8), 8)
        row = tile * 8 - PAD + sub
        in_rows = (row >= -RIM) & (row < rows + RIM) & (row + row_start >= 0) & (row + row_start < row_total)
        for group in range(halves + 2):
            col = (group - 1) * LANES + lane
            inside = (
                in_rows & (col >= -RIM) & (col < cols + RIM)
                & (col + col_start >= 0) & (col + col_start < col_total)
            )
            if group == 0:
                cells = [left_ref[c, at, :] for c in range(CHANS)]
            elif group == halves + 1:
                cells = [right_ref[c, at, :] for c in range(CHANS)]
            else:
                cells = [main_ref[c, at, (group - 1) * LANES : group * LANES] for c in range(CHANS)]
            adjugate, determinant = hermitian_inverse(cells)
            scale = 1.0 / determinant
            for c in range(CHANS):
                feats[c, group, at, :] = jnp.where(inside, cells[c], 0.0)
                feats[CHANS + c, group, at, :] = jnp.where(inside, adjugate[c] * scale, 0.0)
            feats[2 * CHANS, group, at, :] = jnp.where(inside, 1.0, 0.0)
        return 0

    lax.fori_loop(0, row_tiles, features, 0)

    def shifts(turn, _):
        c, tile = turn // row_tiles, turn % row_tiles
        at = pl.ds(pl.multiple_of(tile * 8, 8), 8)
        cells = [feats[c, group, at, :] for group in range(halves + 2)]
        for step in range(-SEARCH, SEARCH + 1):
            for half in range(halves):
                here = cells[half + 1]
                if step > 0:
                    value = pltpu.roll(jnp.where(lane >= step, here, cells[half + 2]), LANES - step, 1)
                elif step < 0:
                    value = pltpu.roll(jnp.where(lane < LANES + step, here, cells[half]), -step, 1)
                else:
                    value = here
                moved[step + SEARCH, c, half, at, :] = value
        near = pltpu.roll(jnp.where(lane >= 96, cells[0], cells[1]), 32, 1)
        far = pltpu.roll(jnp.where(lane >= 96, cells[halves], cells[halves + 1]), 96, 1)
        edges[c, at, :] = jnp.where(lane < 64, near, far)
        return 0

    lax.fori_loop(0, FEATS * row_tiles, shifts, 0)

    def edge_pick(c, _):
        both = jnp.dot(edges[c], pick_ref[...], precision=lax.Precision.HIGHEST, preferred_element_type=f32)
        edge_own[c] = both[:, :LANES]
        edge_other[c] = both[:, LANES:]
        return 0

    lax.fori_loop(0, FEATS, edge_pick, 0)

    def own_tiles(tile, _):
        at = pl.ds(pl.multiple_of(tile * 8, 8), 8)
        for half in range(halves):
            for c in range(FEATS):
                own[c, half, at, :] = gain(c) * feats[partner(c), half + 1, pl.ds(tile * 8 + PAD - PATCH, 8), :]
        return 0

    lax.fori_loop(0, dist_rows // 8, own_tiles, 0)

    def edge_tiles(tile, _):
        at = pl.ds(pl.multiple_of(tile * 8, 8), 8)
        mine = [gain(c) * edge_own[partner(c), pl.ds(tile * 8 + PAD - PATCH, 8), :] for c in range(FEATS)]
        for step in range(SPAN):
            value = None
            for c in range(FEATS):
                term = mine[c] * edge_other[c, pl.ds(tile * 8 + PAD - PATCH - SEARCH + step, 8), :]
                value = term if value is None else value + term
            edge_dist[step, at, :] = value
        return 0

    lax.fori_loop(0, dist_rows // 8, edge_tiles, 0)

    def split(value):
        high = value.astype(bf16)
        return high, (value - high.astype(f32)).astype(bf16)

    def edge_sums(step, _):
        for part in range(rows // 16):
            value = edge_dist[step, pl.ds(16 * part, 16), :]
            for s in range(1, SIDE):
                value = value + edge_dist[step, pl.ds(16 * part + s, 16), :]
            high, low = split(value)
            edge_sum[step, 16 * part : 16 * part + 16, :LANES] = high
            edge_sum[step, 16 * part : 16 * part + 16, LANES:] = low
        return 0

    lax.fori_loop(0, SPAN, edge_sums, 0)
    totals[...] = jnp.zeros_like(totals)
    edge_lane = lax.broadcasted_iota(jnp.int32, (16, LANES), 1)

    def batch(turn, _):
        downs = [offs_ref[turn * BATCH + j, 0] for j in range(BATCH)]
        sides = [offs_ref[turn * BATCH + j, 1] + SEARCH for j in range(BATCH)]

        def distances(tile, _):
            at = pl.ds(pl.multiple_of(tile * 8, 8), 8)
            for half in range(halves):
                mine = [own[c, half, at, :] for c in range(FEATS)]
                for j in range(BATCH):
                    rows_at = pl.ds(tile * 8 + PAD - PATCH + downs[j], 8)
                    value = None
                    for c in range(FEATS):
                        term = mine[c] * moved[sides[j], c, half, rows_at, :]
                        value = term if value is None else value + term
                    dist[j, half, at, :] = value
            return 0

        lax.fori_loop(0, dist_rows // 8, distances, 0)

        def window(j, _):
            down = offs_ref[turn * BATCH + j, 0] + SEARCH
            side = offs_ref[turn * BATCH + j, 1] + SEARCH
            keep = jnp.where(edge_lane // 8 == side, 1.0, 0.0).astype(bf16)
            for part in range(rows // 16):
                at = pl.ds(pl.multiple_of(j * rows + 16 * part, 16), 16)
                for half in range(halves):
                    value = dist[j, half, pl.ds(16 * part, 16), :]
                    for s in range(1, SIDE):
                        value = value + dist[j, half, pl.ds(16 * part + s, 16), :]
                    high, low = split(value)
                    sums[at, half * LANES : (half + 1) * LANES] = high
                    sums[at, cols + half * LANES : cols + (half + 1) * LANES] = low
                for k in range(2):
                    sums[at, 2 * cols + k * LANES : 2 * cols + (k + 1) * LANES] = (
                        edge_sum[down, 16 * part : 16 * part + 16, k * LANES : (k + 1) * LANES] * keep
                    )
            return 0

        lax.fori_loop(0, BATCH, window, 0)

        patch = jnp.dot(sums[...], band_ref[...], preferred_element_type=f32)
        weights[...] = jnp.exp2(patch * EXPONENT)

        def accumulate(tile, _):
            at = pl.ds(pl.multiple_of(tile * 8, 8), 8)
            for half in range(halves):
                total = [totals[c, half, at, :] for c in range(CHANS + 1)]
                for j in range(BATCH):
                    rows_at = pl.ds(tile * 8 + PAD + downs[j], 8)
                    weight = weights[
                        pl.ds(pl.multiple_of(j * rows + tile * 8, 8), 8), half * LANES : (half + 1) * LANES
                    ]
                    for c in range(CHANS):
                        total[c] = total[c] + weight * moved[sides[j], c, half, rows_at, :]
                    total[CHANS] = total[CHANS] + weight * moved[sides[j], 2 * CHANS, half, rows_at, :]
                for c in range(CHANS + 1):
                    totals[c, half, at, :] = total[c]
            return 0

        lax.fori_loop(0, rows // 8, accumulate, 0)
        return 0

    lax.fori_loop(0, offs_ref.shape[0] // BATCH, batch, 0)

    def finish(tile, _):
        at = pl.ds(pl.multiple_of(tile * 8, 8), 8)
        for half in range(halves):
            scale = 1.0 / (1.0 + totals[CHANS, half, at, :])
            for c in range(CHANS):
                out_ref[c, at, half * LANES : (half + 1) * LANES] = (
                    feats[c, half + 1, pl.ds(pl.multiple_of(tile * 8 + PAD, 8), 8), :] + totals[c, half, at, :]
                ) * scale
        return 0

    lax.fori_loop(0, rows // 8, finish, 0)


def exchange(cells, axis, width, dim):
    count = lax.axis_size(axis)
    ends = count - 1
    head = lax.slice_in_dim(cells, 0, width, axis=dim)
    tail = lax.slice_in_dim(cells, cells.shape[dim] - width, cells.shape[dim], axis=dim)
    before = lax.ppermute(tail, axis, [(i, i + 1) for i in range(ends)])
    after = lax.ppermute(head, axis, [(i + 1, i) for i in range(ends)])
    return before, after


def per_device(coherency_field, offsets):
    _, rows, cols = coherency_field.shape
    row_total = rows * lax.axis_size("rows")
    col_total = cols * lax.axis_size("offs")
    origin = jnp.stack([lax.axis_index("rows") * rows, lax.axis_index("offs") * cols]).astype(jnp.int32)
    above, below = exchange(coherency_field, "rows", PAD, 1)
    main = jnp.concatenate([above, coherency_field, below], 1)
    left, right = exchange(main, "offs", RIM, 2)
    left = jnp.pad(left, ((0, 0), (0, 0), (LANES - RIM, 0)))
    right = jnp.pad(right, ((0, 0), (0, 0), (0, LANES - RIM)))
    span_rows = rows + 2 * PAD
    halves = cols // LANES
    vmem = pl.BlockSpec(memory_space=pltpu.VMEM)
    smem = pl.BlockSpec(memory_space=pltpu.SMEM)
    f32, bf16 = jnp.float32, jnp.bfloat16
    return pl.pallas_call(
        functools.partial(despeckle, (rows, cols, row_total, col_total)),
        out_shape=jax.ShapeDtypeStruct((CHANS, rows, cols), f32),
        in_specs=[smem, smem, vmem, vmem, vmem, vmem, vmem],
        out_specs=vmem,
        scratch_shapes=[
            pltpu.VMEM((FEATS, halves + 2, span_rows, LANES), f32),
            pltpu.VMEM((SPAN, FEATS, halves, span_rows, LANES), f32),
            pltpu.VMEM((FEATS, halves, rows + 8, LANES), f32),
            pltpu.VMEM((FEATS, span_rows, LANES), f32),
            pltpu.VMEM((FEATS, span_rows, LANES), f32),
            pltpu.VMEM((FEATS, span_rows, LANES), f32),
            pltpu.VMEM((SPAN, rows + 8, LANES), f32),
            pltpu.VMEM((SPAN, rows, 2 * LANES), bf16),
            pltpu.VMEM((BATCH, halves, rows + 8, LANES), f32),
            pltpu.VMEM((BATCH * rows, 2 * cols + 2 * LANES), bf16),
            pltpu.VMEM((BATCH * rows, cols), f32),
            pltpu.VMEM((CHANS + 1, halves, rows, LANES), f32),
        ],
        compiler_params=pltpu.CompilerParams(vmem_limit_bytes=56 * 1024 * 1024),
    )(
        offsets, origin, main, left, right,
        jnp.asarray(band_matrix(cols), bf16), jnp.asarray(select_matrix(), f32),
    )


def solution(mesh):
    in_specs = (P(None, "rows", "offs"), P())
    out_specs = P(None, "rows", "offs")
    return jax.shard_map(
        per_device, mesh=mesh, in_specs=in_specs, out_specs=out_specs, check_vma=False
    )
```

time: 712 us -> 109 us (0.15)
  the two profiles are of different devices: /device:TPU:1 before, /device:TPU:6 now
where the time goes in v1:
time: 109 us; the launch traced here: 108 us
  Pallas kernels  78.5 us (72%)
  starting transfers between devices  14.9 us (14%)
  waiting for transfers between devices  9.45 us (9%)
  local copies, waits for them, and re-layouts  4.59 us (4%)
    pallas_call x1, Pallas kernels, per_device(): pl.pallas_call(functools.partial(despeckle, (rows, cols, row_total, col_t...  78.5 us
    ppermute x2, starting transfers between devices, exchange(): after = lax.ppermute(head, axis, [(i + 1, i) for i in range(ends)])  8.66 us
    ppermute x2, waiting for transfers between devices, exchange(): before = lax.ppermute(tail, axis, [(i, i + 1) for i in range(ends)])  6.42 us
    ppermute x2, starting transfers between devices, exchange(): before = lax.ppermute(tail, axis, [(i, i + 1) for i in range(ends)])  6.26 us
    ppermute x2, waiting for transfers between devices, exchange(): after = lax.ppermute(head, axis, [(i + 1, i) for i in range(ends)])  3.04 us
  transfers between devices with their start and end apart: 4, of which 4 were waited for; matrix products, arithmetic and copies ran while one was open for 2% of the time, Pallas kernels for 0%

profile of v1, /device:TPU:6, one launch (start us, length us, event | category | flops | bytes accessed | tf_op | source)
XLA Modules:
  0.0 108.2 jit_solution(15385538461755853392)
XLA Ops:
  0.0 0.0 copy-start.1
  0.0 1.1 fusion.1
  1.1 3.8 %collective-permute-start = (f32[9,16,256]{2,1,0:T(8,128)S(1)}, f32[9,16,256]{2,1,0:T(8,128)S(1)}, u32[]{:S(2)}, u32[]{:S(2)}) collective-permute-start(f32[9,16,256]{2,1,0:T(8,128)S(1)} %get-tuple-element.8), channel_id=1, source_target_pairs={{0,4},{4,8},{8,12},{12,16},{16,20},{20,24},{24,28},{28,32},{32,36}... | collective-permute-start | bytes 442376 | tf_op jit(solution)/shard_map/ppermute | solution.py:286
  4.9 6.8 %collective-permute-start.1 = (f32[9,16,256]{2,1,0:T(8,128)S(1)}, f32[9,16,256]{2,1,0:T(8,128)S(1)}, u32[]{:S(2)}, u32[]{:S(2)}) collective-permute-start(f32[9,16,256]{2,1,0:T(8,128)S(1)} %get-tuple-element.7), channel_id=1, source_target_pairs={{4,0},{8,4},{12,8},{16,12},{20,16},{24,20},{28,24},{32,28},{36,32}... | collective-permute-start | bytes 442376 | tf_op jit(solution)/shard_map/ppermute | solution.py:287
  11.7 1.9 %collective-permute-done = f32[9,16,256]{2,1,0:T(8,128)S(1)} collective-permute-done((f32[9,16,256]{2,1,0:T(8,128)S(1)}, f32[9,16,256]{2,1,0:T(8,128)S(1)}, u32[]{:S(2)}, u32[]{:S(2)}) %collective-permute-start) | collective-permute-done | bytes 147488 | tf_op jit(solution)/shard_map/ppermute | solution.py:286
  13.6 0.0 copy-done.1
  13.6 0.1 constant_dynamic-update-slice_fusion.1
  13.7 1.1 %collective-permute-done.1 = f32[9,16,256]{2,1,0:T(8,128)S(1)} collective-permute-done((f32[9,16,256]{2,1,0:T(8,128)S(1)}, f32[9,16,256]{2,1,0:T(8,128)S(1)}, u32[]{:S(2)}, u32[]{:S(2)}) %collective-permute-start.1) | collective-permute-done | bytes 147488 | tf_op jit(solution)/shard_map/ppermute | solution.py:287
  14.8 0.0 copy-start
  14.8 0.2 fusion
  15.0 0.7 copy-done
  15.7 1.9 %collective-permute-start.3 = (f32[9,96,9]{2,1,0:T(8,128)S(1)}, f32[9,96,9]{2,1,0:T(8,128)S(1)}, u32[]{:S(2)}, u32[]{:S(2)}) collective-permute-start(f32[9,96,9]{2,1,0:T(8,128)S(1)} %get-tuple-element.5), channel_id=1, source_target_pairs={{1,0},{2,1},{3,2},{5,4},{6,5},{7,6},{9,8},{10,9},{11,10},{13,12},{... | collective-permute-start | bytes 93320 | tf_op jit(solution)/shard_map/ppermute | solution.py:287
  17.6 2.4 %collective-permute-start.2 = (f32[9,96,9]{2,1,0:T(8,128)S(1)}, f32[9,96,9]{2,1,0:T(8,128)S(1)}, u32[]{:S(2)}, u32[]{:S(2)}) collective-permute-start(f32[9,96,9]{2,1,0:T(8,128)S(1)} %get-tuple-element.6), channel_id=1, source_target_pairs={{0,1},{1,2},{2,3},{4,5},{5,6},{6,7},{8,9},{9,10},{10,11},{12,13},{... | collective-permute-start | bytes 93320 | tf_op jit(solution)/shard_map/ppermute | solution.py:286
  20.1 0.0 copy-start.2
  20.1 0.7 pad_add_fusion.origin_ref
  20.7 0.0 copy-done.2
  20.7 0.7 copy.5.offs_ref
  21.5 1.9 %collective-permute-done.3 = f32[9,96,9]{2,1,0:T(8,128)S(1)} collective-permute-done((f32[9,96,9]{2,1,0:T(8,128)S(1)}, f32[9,96,9]{2,1,0:T(8,128)S(1)}, u32[]{:S(2)}, u32[]{:S(2)}) %collective-permute-start.3) | collective-permute-done | bytes 31136 | tf_op jit(solution)/shard_map/ppermute | solution.py:287
  23.4 0.8 pad.9.right_ref
  24.2 4.5 %collective-permute-done.2 = f32[9,96,9]{2,1,0:T(8,128)S(1)} collective-permute-done((f32[9,96,9]{2,1,0:T(8,128)S(1)}, f32[9,96,9]{2,1,0:T(8,128)S(1)}, u32[]{:S(2)}, u32[]{:S(2)}) %collective-permute-start.2) | collective-permute-done | bytes 31136 | tf_op jit(solution)/shard_map/ppermute | solution.py:286
  28.8 1.0 pad.8.left_ref
  29.7 78.5 %shard_map.46 = f32[9,64,256]{2,1,0:T(8,128)} custom-call(s32[120,2]{1,0:T(8,128)} %copy.5.offs_ref, s32[2]{0:T(128)} %pad_add_fusion.origin_ref, f32[9,96,256]{2,1,0:T(8,128)} %copy-done, f32[9,96,128]{2,1,0:T(8,128)} %pad.8.left_ref, f32[9,96,128]{2,1,0:T(8,128)} %pad.9.right_ref, bf16[768,256]{1,0:T(8,128)(2,1)} %constant.20.clone.band_ref, ...), custom_call_target="tpu_custom_call" | custom-call | tf_op jit(solution)/shard_map/pallas_call | solution.py:306
  (2 shorter events, 0.0 us)
Async XLA Ops:
  0.0 13.6 %copy-start.1 = (f32[9,64,256]{2,1,0:T(8,128)S(1)}, f32[9,64,256]{2,1,0:T(8,128)}, u32[]{:S(2)}) copy-start(f32[9,64,256]{2,1,0:T(8,128)} %param.4) | copy-start | bytes 1769476
  1.1 12.5 %collective-permute-start = (f32[9,16,256]{2,1,0:T(8,128)S(1)}, f32[9,16,256]{2,1,0:T(8,128)S(1)}, u32[]{:S(2)}, u32[]{:S(2)}) collective-permute-start(f32[9,16,256]{2,1,0:T(8,128)S(1)} %get-tuple-element.8), channel_id=1, source_target_pairs={{0,4},{4,8},{8,12},{12,16},{16,20},{20,24},{24,28},{28,32},{32,36}... | collective-permute-start | bytes 442376 | tf_op jit(solution)/shard_map/ppermute | solution.py:286
  4.9 9.8 %collective-permute-start.1 = (f32[9,16,256]{2,1,0:T(8,128)S(1)}, f32[9,16,256]{2,1,0:T(8,128)S(1)}, u32[]{:S(2)}, u32[]{:S(2)}) collective-permute-start(f32[9,16,256]{2,1,0:T(8,128)S(1)} %get-tuple-element.7), channel_id=1, source_target_pairs={{4,0},{8,4},{12,8},{16,12},{20,16},{24,20},{28,24},{32,28},{36,32}... | collective-permute-start | bytes 442376 | tf_op jit(solution)/shard_map/ppermute | solution.py:287
  14.8 0.9 copy-start
  15.7 7.7 %collective-permute-start.3 = (f32[9,96,9]{2,1,0:T(8,128)S(1)}, f32[9,96,9]{2,1,0:T(8,128)S(1)}, u32[]{:S(2)}, u32[]{:S(2)}) collective-permute-start(f32[9,96,9]{2,1,0:T(8,128)S(1)} %get-tuple-element.5), channel_id=1, source_target_pairs={{1,0},{2,1},{3,2},{5,4},{6,5},{7,6},{9,8},{10,9},{11,10},{13,12},{... | collective-permute-start | bytes 93320 | tf_op jit(solution)/shard_map/ppermute | solution.py:287
  17.6 11.1 %collective-permute-start.2 = (f32[9,96,9]{2,1,0:T(8,128)S(1)}, f32[9,96,9]{2,1,0:T(8,128)S(1)}, u32[]{:S(2)}, u32[]{:S(2)}) collective-permute-start(f32[9,96,9]{2,1,0:T(8,128)S(1)} %get-tuple-element.6), channel_id=1, source_target_pairs={{0,1},{1,2},{2,3},{4,5},{5,6},{6,7},{8,9},{9,10},{10,11},{12,13},{... | collective-permute-start | bytes 93320 | tf_op jit(solution)/shard_map/ppermute | solution.py:286
  20.1 0.7 copy-start.2

commit v2 on v1

--- a/solution.py
+++ b/solution.py
@@ -19,7 +19,8 @@
 PAD = 16
 CHANS = 9
 FEATS = 2 * CHANS + 1
-BATCH = 8
+BATCH = 24
+BANKS = 16
 EXPONENT = -math.log2(math.e) / (STRENGTH * SIDE * SIDE)
 
 
@@ -77,7 +78,7 @@
             lane = 32 + place - PATCH if place < PATCH else 96 + place - PATCH
             pick[lane, 8 * turn + place] = 1.0
             pick[lane + turn - SEARCH, LANES + 8 * turn + place] = 1.0
-    return pick
+    return np.concatenate([pick] * 3, 0)
 
 
 def gain(feature):
@@ -93,7 +94,7 @@
 
 
 def despeckle(
-    sizes, offs_ref, origin_ref, main_ref, left_ref, right_ref, band_ref, pick_ref, out_ref,
+    sizes, offs_ref, origin_ref, field_ref, above_ref, below_ref, left_ref, right_ref, band_ref, pick_ref, out_ref,
     feats, moved, own, edges, edge_own, edge_other, edge_dist, edge_sum, dist, sums, weights, totals,
 ):
     rows, cols, row_total, col_total = sizes
@@ -106,8 +107,9 @@
     row_start, col_start = origin_ref[0], origin_ref[1]
     f32, bf16 = jnp.float32, jnp.bfloat16
 
-    def features(tile, _):
+    def features(source_ref, first, tile, _):
         at = pl.ds(pl.multiple_of(tile * 8, 8), 8)
+        source_at = pl.ds(pl.multiple_of(tile * 8 - first, 8), 8)
         row = tile * 8 - PAD + sub
         in_rows = (row >= -RIM) & (row < rows + RIM) & (row + row_start >= 0) & (row + row_start < row_total)
         for group in range(halves + 2):
@@ -117,46 +119,59 @@
                 & (col + col_start >= 0) & (col + col_start < col_total)
             )
             if group == 0:
-                cells = [left_ref[c, at, :] for c in range(CHANS)]
+                packed = left_ref[at, :]
+                cells = [pltpu.roll(packed, LANES - RIM - RIM * c, 1) for c in range(CHANS)]
             elif group == halves + 1:
-                cells = [right_ref[c, at, :] for c in range(CHANS)]
+                packed = right_ref[at, :]
+                cells = [pltpu.roll(packed, LANES - RIM * c, 1) if c else packed for c in range(CHANS)]
             else:
-                cells = [main_ref[c, at, (group - 1) * LANES : group * LANES] for c in range(CHANS)]
+                cells = [source_ref[c, source_at, (group - 1) * LANES : group * LANES] for c in range(CHANS)]
             adjugate, determinant = hermitian_inverse(cells)
             scale = 1.0 / determinant
             for c in range(CHANS):
-                feats[c, group, at, :] = jnp.where(inside, cells[c], 0.0)
-                feats[CHANS + c, group, at, :] = jnp.where(inside, adjugate[c] * scale, 0.0)
-            feats[2 * CHANS, group, at, :] = jnp.where(inside, 1.0, 0.0)
-        return 0
-
-    lax.fori_loop(0, row_tiles, features, 0)
-
-    def shifts(turn, _):
-        c, tile = turn // row_tiles, turn % row_tiles
+                feats[group, c, at, :] = jnp.where(inside, cells[c], 0.0)
+                feats[group, CHANS + c, at, :] = jnp.where(inside, adjugate[c] * scale, 0.0)
+            feats[group, 2 * CHANS, at, :] = jnp.where(inside, 1.0, 0.0)
+        return 0
+
+    head, tail = PAD // 8, (PAD + rows) // 8
+    lax.fori_loop(0, head, functools.partial(features, above_ref, 0), 0)
+    lax.fori_loop(head, tail, functools.partial(features, field_ref, PAD), 0)
+    lax.fori_loop(tail, row_tiles, functools.partial(features, below_ref, PAD + rows), 0)
+
+    def split(value):
+        high = value.astype(bf16)
+        return high, (value - high.astype(f32)).astype(bf16)
+
+    def shifts(tile, _):
         at = pl.ds(pl.multiple_of(tile * 8, 8), 8)
-        cells = [feats[c, group, at, :] for group in range(halves + 2)]
-        for step in range(-SEARCH, SEARCH + 1):
-            for half in range(halves):
-                here = cells[half + 1]
-                if step > 0:
-                    value = pltpu.roll(jnp.where(lane >= step, here, cells[half + 2]), LANES - step, 1)
-                elif step < 0:
-                    value = pltpu.roll(jnp.where(lane < LANES + step, here, cells[half]), -step, 1)
-                else:
-                    value = here
-                moved[step + SEARCH, c, half, at, :] = value
-        near = pltpu.roll(jnp.where(lane >= 96, cells[0], cells[1]), 32, 1)
-        far = pltpu.roll(jnp.where(lane >= 96, cells[halves], cells[halves + 1]), 96, 1)
-        edges[c, at, :] = jnp.where(lane < 64, near, far)
-        return 0
-
-    lax.fori_loop(0, FEATS * row_tiles, shifts, 0)
+        for c in range(FEATS):
+            cells = [feats[group, c, at, :] for group in range(halves + 2)]
+            for step in range(-SEARCH, SEARCH + 1):
+                for half in range(halves):
+                    here = cells[half + 1]
+                    if step > 0:
+                        value = pltpu.roll(jnp.where(lane >= step, here, cells[half + 2]), LANES - step, 1)
+                    elif step < 0:
+                        value = pltpu.roll(jnp.where(lane < LANES + step, here, cells[half]), -step, 1)
+                    else:
+                        value = here
+                    moved[step + SEARCH, half, c, at, :] = value
+            near = pltpu.roll(jnp.where(lane >= 96, cells[0], cells[1]), 32, 1)
+            far = pltpu.roll(jnp.where(lane >= 96, cells[halves], cells[halves + 1]), 96, 1)
+            edges[pl.ds(pl.multiple_of(c * span_rows + tile * 8, 8), 8), :] = jnp.where(lane < 64, near, far)
+        return 0
+
+    lax.fori_loop(0, row_tiles, shifts, 0)
 
     def edge_pick(c, _):
-        both = jnp.dot(edges[c], pick_ref[...], precision=lax.Precision.HIGHEST, preferred_element_type=f32)
-        edge_own[c] = both[:, :LANES]
-        edge_other[c] = both[:, LANES:]
+        value = edges[pl.ds(pl.multiple_of(c * span_rows, 8), span_rows), :]
+        high, rest = value.astype(bf16), value - value.astype(bf16).astype(f32)
+        middle, low = split(rest)
+        parts = jnp.concatenate([high, middle, low], 1)
+        both = jnp.dot(parts, pick_ref[...], preferred_element_type=f32)
+        edge_own[c, :span_rows] = both[:, :LANES]
+        edge_other[c, :span_rows] = both[:, LANES:]
         return 0
 
     lax.fori_loop(0, FEATS, edge_pick, 0)
@@ -165,7 +180,7 @@
         at = pl.ds(pl.multiple_of(tile * 8, 8), 8)
         for half in range(halves):
             for c in range(FEATS):
-                own[c, half, at, :] = gain(c) * feats[partner(c), half + 1, pl.ds(tile * 8 + PAD - PATCH, 8), :]
+                own[half, c, at, :] = gain(c) * feats[half + 1, partner(c), pl.ds(tile * 8 + PAD - PATCH, 8), :]
         return 0
 
     lax.fori_loop(0, dist_rows // 8, own_tiles, 0)
@@ -183,10 +198,6 @@
 
     lax.fori_loop(0, dist_rows // 8, edge_tiles, 0)
 
-    def split(value):
-        high = value.astype(bf16)
-        return high, (value - high.astype(f32)).astype(bf16)
-
     def edge_sums(step, _):
         for part in range(rows // 16):
             value = edge_dist[step, pl.ds(16 * part, 16), :]
@@ -205,20 +216,20 @@
         downs = [offs_ref[turn * BATCH + j, 0] for j in range(BATCH)]
         sides = [offs_ref[turn * BATCH + j, 1] + SEARCH for j in range(BATCH)]
 
-        def distances(tile, _):
+        def distances(step, _):
+            half, tile = step % halves, step // halves
             at = pl.ds(pl.multiple_of(tile * 8, 8), 8)
-            for half in range(halves):
-                mine = [own[c, half, at, :] for c in range(FEATS)]
-                for j in range(BATCH):
-                    rows_at = pl.ds(tile * 8 + PAD - PATCH + downs[j], 8)
-                    value = None
-                    for c in range(FEATS):
-                        term = mine[c] * moved[sides[j], c, half, rows_at, :]
-                        value = term if value is None else value + term
-                    dist[j, half, at, :] = value
+            mine = [own[half, c, at, :] for c in range(FEATS)]
+            for j in range(BATCH):
+                rows_at = pl.ds(tile * 8 + PAD - PATCH + downs[j], 8)
+                value = None
+                for c in range(FEATS):
+                    term = mine[c] * moved[sides[j], half, c, rows_at, :]
+                    value = term if value is None else value + term
+                dist[j, half, at, :] = value
             return 0
 
-        lax.fori_loop(0, dist_rows // 8, distances, 0)
+        lax.fori_loop(0, halves * dist_rows // 8, distances, 0)
 
         def window(j, _):
             down = offs_ref[turn * BATCH + j, 0] + SEARCH
@@ -247,17 +258,17 @@
         def accumulate(tile, _):
             at = pl.ds(pl.multiple_of(tile * 8, 8), 8)
             for half in range(halves):
-                total = [totals[c, half, at, :] for c in range(CHANS + 1)]
+                total = [totals[half, c, at, :] for c in range(CHANS + 1)]
                 for j in range(BATCH):
                     rows_at = pl.ds(tile * 8 + PAD + downs[j], 8)
                     weight = weights[
                         pl.ds(pl.multiple_of(j * rows + tile * 8, 8), 8), half * LANES : (half + 1) * LANES
                     ]
                     for c in range(CHANS):
-                        total[c] = total[c] + weight * moved[sides[j], c, half, rows_at, :]
-                    total[CHANS] = total[CHANS] + weight * moved[sides[j], 2 * CHANS, half, rows_at, :]
+                        total[c] = total[c] + weight * moved[sides[j], half, c, rows_at, :]
+                    total[CHANS] = total[CHANS] + weight * moved[sides[j], half, 2 * CHANS, rows_at, :]
                 for c in range(CHANS + 1):
-                    totals[c, half, at, :] = total[c]
+                    totals[half, c, at, :] = total[c]
             return 0
 
         lax.fori_loop(0, rows // 8, accumulate, 0)
@@ -268,65 +279,117 @@
     def finish(tile, _):
         at = pl.ds(pl.multiple_of(tile * 8, 8), 8)
         for half in range(halves):
-            scale = 1.0 / (1.0 + totals[CHANS, half, at, :])
+            span = slice(half * LANES, (half + 1) * LANES)
+            scale = 1.0 / (1.0 + totals[half, CHANS, at, :])
             for c in range(CHANS):
-                out_ref[c, at, half * LANES : (half + 1) * LANES] = (
-                    feats[c, half + 1, pl.ds(pl.multiple_of(tile * 8 + PAD, 8), 8), :] + totals[c, half, at, :]
-                ) * scale
+                out_ref[c, at, span] = (field_ref[c, at, span] + totals[half, c, at, :]) * scale
         return 0
 
     lax.fori_loop(0, rows // 8, finish, 0)
 
 
-def exchange(cells, axis, width, dim):
-    count = lax.axis_size(axis)
-    ends = count - 1
-    head = lax.slice_in_dim(cells, 0, width, axis=dim)
-    tail = lax.slice_in_dim(cells, cells.shape[dim] - width, cells.shape[dim], axis=dim)
-    before = lax.ppermute(tail, axis, [(i, i + 1) for i in range(ends)])
-    after = lax.ppermute(head, axis, [(i + 1, i) for i in range(ends)])
-    return before, after
-
-
-def per_device(coherency_field, offsets):
-    _, rows, cols = coherency_field.shape
-    row_total = rows * lax.axis_size("rows")
-    col_total = cols * lax.axis_size("offs")
-    origin = jnp.stack([lax.axis_index("rows") * rows, lax.axis_index("offs") * cols]).astype(jnp.int32)
-    above, below = exchange(coherency_field, "rows", PAD, 1)
-    main = jnp.concatenate([above, coherency_field, below], 1)
-    left, right = exchange(main, "offs", RIM, 2)
-    left = jnp.pad(left, ((0, 0), (0, 0), (LANES - RIM, 0)))
-    right = jnp.pad(right, ((0, 0), (0, 0), (0, LANES - RIM)))
+def swap_halo(field_ref, above_ref, below_ref, left_ref, right_ref, packs, send_sems, recv_sems):
+    rows, cols = field_ref.shape[1:]
+    row, col = lax.axis_index("rows"), lax.axis_index("offs")
+    row_count, col_count = lax.axis_size("rows"), lax.axis_size("offs")
+
+    def device(down, side):
+        return (lax.rem(row + down + row_count, row_count), lax.rem(col + side + col_count, col_count))
+
+    around = [(down, side) for down in (-1, 0, 1) for side in (-1, 0, 1) if (down, side) != (0, 0)]
+    barrier = pltpu.get_barrier_semaphore()
+    for down, side in around:
+        pl.semaphore_signal(barrier, inc=1, device_id=device(down, side), device_id_type=pl.DeviceIdType.MESH)
+
+    lane = lax.broadcasted_iota(jnp.int32, (rows, LANES), 1)
+    first = field_ref[0, :, :LANES]
+    last = pltpu.roll(field_ref[0, :, cols - LANES :], RIM, 1)
+    for c in range(1, CHANS):
+        here = (lane >= RIM * c) & (lane < RIM * (c + 1))
+        first = jnp.where(here, pltpu.roll(field_ref[c, :, :LANES], RIM * c, 1), first)
+        last = jnp.where(here, pltpu.roll(field_ref[c, :, cols - LANES :], (RIM * c + RIM) % LANES, 1), last)
+    packs[0] = first
+    packs[1] = last
+    pl.semaphore_wait(barrier, len(around))
+
+    copies = []
+    for k, (down, side) in enumerate(around):
+        start, size, put = {-1: (0, PAD, PAD + rows), 0: (0, rows, PAD), 1: (rows - PAD, PAD, 0)}[down]
+        if side == 0:
+            source = field_ref.at[:, start : start + size, :]
+            target = below_ref if down < 0 else above_ref
+        else:
+            source = packs.at[0 if side < 0 else 1, start : start + size, :]
+            target = (right_ref if side < 0 else left_ref).at[put : put + size, :]
+        copies.append(pltpu.make_async_remote_copy(
+            src_ref=source, dst_ref=target, send_sem=send_sems.at[k], recv_sem=recv_sems.at[k],
+            device_id=device(down, side), device_id_type=pl.DeviceIdType.MESH,
+        ))
+    for copy in copies:
+        copy.start()
+    for copy in copies:
+        copy.wait()
+
+
+def exchange(field):
+    _, rows, cols = field.shape
+    vmem = pl.BlockSpec(memory_space=pltpu.VMEM)
+    slab = jax.ShapeDtypeStruct((CHANS, PAD, cols), jnp.float32)
+    side = jax.ShapeDtypeStruct((rows + 2 * PAD, LANES), jnp.float32)
+    return pl.pallas_call(
+        swap_halo,
+        out_shape=(slab, slab, side, side),
+        in_specs=[vmem],
+        out_specs=(vmem, vmem, vmem, vmem),
+        scratch_shapes=[
+            pltpu.VMEM((2, rows, LANES), jnp.float32),
+            pltpu.SemaphoreType.DMA((8,)),
+            pltpu.SemaphoreType.DMA((8,)),
+        ],
+        compiler_params=pltpu.CompilerParams(collective_id=0, has_side_effects=True),
+    )(field)
+
+
+def filter_block(sizes, offsets, origin, field, above, below, left, right):
+    rows, cols = sizes[:2]
     span_rows = rows + 2 * PAD
     halves = cols // LANES
     vmem = pl.BlockSpec(memory_space=pltpu.VMEM)
     smem = pl.BlockSpec(memory_space=pltpu.SMEM)
     f32, bf16 = jnp.float32, jnp.bfloat16
     return pl.pallas_call(
-        functools.partial(despeckle, (rows, cols, row_total, col_total)),
+        functools.partial(despeckle, sizes),
         out_shape=jax.ShapeDtypeStruct((CHANS, rows, cols), f32),
-        in_specs=[smem, smem, vmem, vmem, vmem, vmem, vmem],
+        in_specs=[smem, smem] + [vmem] * 7,
         out_specs=vmem,
         scratch_shapes=[
-            pltpu.VMEM((FEATS, halves + 2, span_rows, LANES), f32),
-            pltpu.VMEM((SPAN, FEATS, halves, span_rows, LANES), f32),
-            pltpu.VMEM((FEATS, halves, rows + 8, LANES), f32),
-            pltpu.VMEM((FEATS, span_rows, LANES), f32),
-            pltpu.VMEM((FEATS, span_rows, LANES), f32),
-            pltpu.VMEM((FEATS, span_rows, LANES), f32),
+            pltpu.VMEM((halves + 2, FEATS, span_rows + BANKS, LANES), f32),
+            pltpu.VMEM((SPAN, halves, FEATS, span_rows + BANKS, LANES), f32),
+            pltpu.VMEM((halves, FEATS, rows + BANKS, LANES), f32),
+            pltpu.VMEM((FEATS * span_rows, LANES), f32),
+            pltpu.VMEM((FEATS, span_rows + BANKS, LANES), f32),
+            pltpu.VMEM((FEATS, span_rows + BANKS, LANES), f32),
             pltpu.VMEM((SPAN, rows + 8, LANES), f32),
             pltpu.VMEM((SPAN, rows, 2 * LANES), bf16),
             pltpu.VMEM((BATCH, halves, rows + 8, LANES), f32),
             pltpu.VMEM((BATCH * rows, 2 * cols + 2 * LANES), bf16),
             pltpu.VMEM((BATCH * rows, cols), f32),
-            pltpu.VMEM((CHANS + 1, halves, rows, LANES), f32),
+            pltpu.VMEM((halves, CHANS + 1, rows + BANKS, LANES), f32),
         ],
         compiler_params=pltpu.CompilerParams(vmem_limit_bytes=56 * 1024 * 1024),
     )(
-        offsets, origin, main, left, right,
-        jnp.asarray(band_matrix(cols), bf16), jnp.asarray(select_matrix(), f32),
+        offsets, origin, field, above, below, left, right,
+        jnp.asarray(band_matrix(cols), bf16), jnp.asarray(select_matrix(), bf16),
     )
+
+
+def per_device(coherency_field, offsets):
+    _, rows, cols = coherency_field.shape
+    row_total = rows * lax.axis_size("rows")
+    col_total = cols * lax.axis_size("offs")
+    origin = jnp.stack([lax.axis_index("rows") * rows, lax.axis_index("offs") * cols]).astype(jnp.int32)
+    halo = exchange(coherency_field)
+    return filter_block((rows, cols, row_total, col_total), offsets, origin, coherency_field, *halo)
 
 
 def solution(mesh):

time: 109 us -> 67.8 us (0.62)
  the two profiles are of different devices: /device:TPU:6 before, /device:TPU:1 now
where the time goes in v2:
time: 67.8 us; the launch traced here: 67.6 us
  Pallas kernels  66.2 us (98%)
  local copies, waits for them, and re-layouts  0.81 us (1%)
    pallas_call x1, Pallas kernels, filter_block(): pl.pallas_call(functools.partial(despeckle, sizes), out_shape=jax.ShapeDt...  48 us
    pallas_call x1, Pallas kernels, exchange(): pl.pallas_call(swap_halo, out_shape=(slab, slab, side, side), in_specs=[v...  18.2 us

profile of v2, /device:TPU:1, one launch (start us, length us, event | category | flops | bytes accessed | tf_op | source)
XLA Modules:
  0.0 67.6 jit_solution(10791678835123879470)
XLA Ops:
  0.0 0.0 copy-start
  0.0 0.6 pad_add_fusion.origin_ref
  0.6 0.1 copy-done
  0.7 0.7 %copy.5.offs_ref = s32[120,2]{1,0:T(8,128)} copy(s32[120,2]{0,1:T(2,128)S(1)} %copy-done) | data formatting | bytes 1920 | tf_op args[1]
  1.4 18.2 %shard_map.46 = (f32[9,16,256]{2,1,0:T(8,128)}, f32[9,16,256]{2,1,0:T(8,128)}, f32[96,128]{1,0:T(8,128)}, f32[96,128]{1,0:T(8,128)}) custom-call(f32[9,64,256]{2,1,0:T(8,128)} %field_ref.3), custom_call_target="tpu_custom_call" | custom-call | tf_op jit(solution)/shard_map/pallas_call | solution.py:339
  19.6 48.0 %shard_map.47 = f32[9,64,256]{2,1,0:T(8,128)} custom-call(s32[120,2]{1,0:T(8,128)} %copy.5.offs_ref, s32[2]{0:T(128)} %pad_add_fusion.origin_ref, f32[9,64,256]{2,1,0:T(8,128)} %field_ref.3, f32[9,16,256]{2,1,0:T(8,128)} %get-tuple-element.9.above_ref, f32[9,16,256]{2,1,0:T(8,128)} %get-tuple-element.10.below_ref, f32[96,128]{1,0:T(8,128)} %get-tuple-element.11.left_ref, ...), custom_call_target="tpu_custom_call" | custom-call | tf_op jit(solution)/shard_map/pallas_call | solution.py:360
Async XLA Ops:
  0.0 0.7 %copy-start = (s32[120,2]{0,1:T(2,128)S(1)}, s32[120,2]{0,1:T(2,128)}, u32[]{:S(2)}) copy-start(s32[120,2]{0,1:T(2,128)} %param.5) | copy-start | bytes 2884

commit v3 on v2

--- a/solution.py
+++ b/solution.py
@@ -94,8 +94,8 @@
 
 
 def despeckle(
-    sizes, offs_ref, origin_ref, field_ref, above_ref, below_ref, left_ref, right_ref, band_ref, pick_ref, out_ref,
-    feats, moved, own, edges, edge_own, edge_other, edge_dist, edge_sum, dist, sums, weights, totals,
+    sizes, offs_ref, field_ref, band_ref, pick_ref, out_ref,
+    above_ref, below_ref, left_ref, right_ref, packs, send_sems, recv_sems, feats, moved, own, edges, edge_own, edge_other, edge_dist, edge_sum, dist, sums, weights, totals,
 ):
     rows, cols, row_total, col_total = sizes
     span_rows = rows + 2 * PAD
@@ -104,7 +104,8 @@
     dist_rows = rows + 8
     lane = lax.broadcasted_iota(jnp.int32, (8, LANES), 1)
     sub = lax.broadcasted_iota(jnp.int32, (8, LANES), 0)
-    row_start, col_start = origin_ref[0], origin_ref[1]
+    row_start, col_start = lax.axis_index("rows") * rows, lax.axis_index("offs") * cols
+    swap_halo(field_ref, above_ref, below_ref, left_ref, right_ref, packs, send_sems, recv_sems)
     f32, bf16 = jnp.float32, jnp.bfloat16
 
     def features(source_ref, first, tile, _):
@@ -331,26 +332,7 @@
         copy.wait()
 
 
-def exchange(field):
-    _, rows, cols = field.shape
-    vmem = pl.BlockSpec(memory_space=pltpu.VMEM)
-    slab = jax.ShapeDtypeStruct((CHANS, PAD, cols), jnp.float32)
-    side = jax.ShapeDtypeStruct((rows + 2 * PAD, LANES), jnp.float32)
-    return pl.pallas_call(
-        swap_halo,
-        out_shape=(slab, slab, side, side),
-        in_specs=[vmem],
-        out_specs=(vmem, vmem, vmem, vmem),
-        scratch_shapes=[
-            pltpu.VMEM((2, rows, LANES), jnp.float32),
-            pltpu.SemaphoreType.DMA((8,)),
-            pltpu.SemaphoreType.DMA((8,)),
-        ],
-        compiler_params=pltpu.CompilerParams(collective_id=0, has_side_effects=True),
-    )(field)
-
-
-def filter_block(sizes, offsets, origin, field, above, below, left, right):
+def filter_block(sizes, offsets, field):
     rows, cols = sizes[:2]
     span_rows = rows + 2 * PAD
     halves = cols // LANES
@@ -360,9 +342,16 @@
     return pl.pallas_call(
         functools.partial(despeckle, sizes),
         out_shape=jax.ShapeDtypeStruct((CHANS, rows, cols), f32),
-        in_specs=[smem, smem] + [vmem] * 7,
+        in_specs=[smem] + [vmem] * 3,
         out_specs=vmem,
         scratch_shapes=[
+            pltpu.VMEM((CHANS, PAD, cols), f32),
+            pltpu.VMEM((CHANS, PAD, cols), f32),
+            pltpu.VMEM((span_rows, LANES), f32),
+            pltpu.VMEM((span_rows, LANES), f32),
+            pltpu.VMEM((2, rows, LANES), f32),
+            pltpu.SemaphoreType.DMA((8,)),
+            pltpu.SemaphoreType.DMA((8,)),
             pltpu.VMEM((halves + 2, FEATS, span_rows + BANKS, LANES), f32),
             pltpu.VMEM((SPAN, halves, FEATS, span_rows + BANKS, LANES), f32),
             pltpu.VMEM((halves, FEATS, rows + BANKS, LANES), f32),
@@ -376,10 +365,11 @@
             pltpu.VMEM((BATCH * rows, cols), f32),
             pltpu.VMEM((halves, CHANS + 1, rows + BANKS, LANES), f32),
         ],
-        compiler_params=pltpu.CompilerParams(vmem_limit_bytes=56 * 1024 * 1024),
+        compiler_params=pltpu.CompilerParams(
+            vmem_limit_bytes=56 * 1024 * 1024, collective_id=0, has_side_effects=True
+        ),
     )(
-        offsets, origin, field, above, below, left, right,
-        jnp.asarray(band_matrix(cols), bf16), jnp.asarray(select_matrix(), bf16),
+        offsets, field, jnp.asarray(band_matrix(cols), bf16), jnp.asarray(select_matrix(), bf16),
     )
 
 
@@ -387,9 +377,7 @@
     _, rows, cols = coherency_field.shape
     row_total = rows * lax.axis_size("rows")
     col_total = cols * lax.axis_size("offs")
-    origin = jnp.stack([lax.axis_index("rows") * rows, lax.axis_index("offs") * cols]).astype(jnp.int32)
-    halo = exchange(coherency_field)
-    return filter_block((rows, cols, row_total, col_total), offsets, origin, coherency_field, *halo)
+    return filter_block((rows, cols, row_total, col_total), offsets, coherency_field)
 
 
 def solution(mesh):

time: 67.8 us -> 68.1 us (level)
  local copies, waits for them, and re-layouts: 0.81 us -> 3.32 us
  Pallas kernels: 66.2 us -> 64.5 us
    pallas_call x1 -> x0, Pallas kernels: 18.2 us -> none  [exchange(): pl.pallas_call(swap_halo, out_shape=(slab, slab, side, side), in_specs=[v...]
    pallas_call x1, Pallas kernels: 48 us -> 64.5 us  [filter_block(): pl.pallas_call(functools.partial(despeckle, sizes), out_shape=jax.ShapeDt...]
    unnamed x3 -> x2, local copies, waits for them, and re-layouts: 0.81 us -> 3.32 us
where the time goes in v3:
time: 68.1 us; the launch traced here: 67.9 us
  Pallas kernels  64.5 us (95%)
  local copies, waits for them, and re-layouts  3.32 us (5%)
    pallas_call x1, Pallas kernels, filter_block(): pl.pallas_call(functools.partial(despeckle, sizes), out_shape=jax.ShapeDt...  64.5 us
    unnamed x2, local copies, waits for them, and re-layouts  3.32 us

profile of v3, /device:TPU:1, one launch (start us, length us, event | category | flops | bytes accessed | tf_op | source)
XLA Modules:
  0.0 67.9 jit_solution(16389143183334281287)
XLA Ops:
  0.0 1.4 %copy.5.offs_ref = s32[120,2]{1,0:T(8,128)} copy(s32[120,2]{0,1:T(2,128)} %param.5) | data formatting | bytes 1920 | tf_op args[1]
  1.4 64.5 %shard_map.46 = f32[9,64,256]{2,1,0:T(8,128)} custom-call(s32[120,2]{1,0:T(8,128)} %copy.5.offs_ref, f32[9,64,256]{2,1,0:T(8,128)} %field_ref.1, bf16[768,256]{1,0:T(8,128)(2,1)} %constant.4.clone.band_ref, bf16[384,256]{1,0:T(8,128)(2,1)} %constant.5.clone.pick_ref), custom_call_target="tpu_custom_call" | custom-call | tf_op jit(solution)/shard_map/pallas_call | solution.py:342
  66.0 1.9 %copy.7 = f32[9,64,256]{2,1,0:T(8,128)} copy(f32[9,64,256]{2,1,0:T(8,128)} %shard_map.46) | data formatting | bytes 1179648

commit v4 on v3

v4 whole, which is shorter than its diff:
```python
import functools
import math

import jax
import jax.numpy as jnp
import numpy as np
from jax import lax
from jax.experimental import pallas as pl
from jax.experimental.pallas import tpu as pltpu
from jax.sharding import PartitionSpec as P

SEARCH = 6
PATCH = 3
SIDE = 2 * PATCH + 1
SPAN = 2 * SEARCH + 1
RIM = SEARCH + PATCH
STRENGTH = 1.5
LANES = 128
PAD = 16
CHANS = 9
FEATS = 2 * CHANS + 1
BATCH = 24
GROUP = 12
BANKS = 16
EXPONENT = -math.log2(math.e) / (STRENGTH * SIDE * SIDE)


def hermitian_inverse(matrix):
    diag_one, diag_two, diag_three = matrix[0], matrix[1], matrix[2]
    re_onetwo, re_onethree, re_twothree = matrix[3], matrix[4], matrix[5]
    im_onetwo, im_onethree, im_twothree = matrix[6], matrix[7], matrix[8]
    abs_onetwo = re_onetwo * re_onetwo + im_onetwo * im_onetwo
    abs_onethree = re_onethree * re_onethree + im_onethree * im_onethree
    abs_twothree = re_twothree * re_twothree + im_twothree * im_twothree
    yz_real = re_onethree * re_twothree + im_onethree * im_twothree
    yz_imag = im_onethree * re_twothree - re_onethree * im_twothree
    xz_real = re_onetwo * re_twothree - im_onetwo * im_twothree
    xz_imag = re_onetwo * im_twothree + im_onetwo * re_twothree
    yx_real = re_onethree * re_onetwo + im_onethree * im_onetwo
    yx_imag = im_onethree * re_onetwo - re_onethree * im_onetwo
    triple_real = xz_real * re_onethree + xz_imag * im_onethree
    determinant = (
        diag_one * diag_two * diag_three
        + 2.0 * triple_real
        - diag_one * abs_twothree
        - diag_two * abs_onethree
        - diag_three * abs_onetwo
    )
    adjugate = [
        diag_two * diag_three - abs_twothree,
        diag_one * diag_three - abs_onethree,
        diag_one * diag_two - abs_onetwo,
        -(re_onetwo * diag_three - yz_real),
        xz_real - re_onethree * diag_two,
        -(diag_one * re_twothree - yx_real),
        -(im_onetwo * diag_three - yz_imag),
        xz_imag - im_onethree * diag_two,
        -(diag_one * im_twothree - yx_imag),
    ]
    return adjugate, determinant


def edge_pairs(cols):
    pairs = []
    for step in range(-SEARCH, SEARCH + 1):
        for column in range(-PATCH, cols + PATCH):
            if not (0 <= column < cols and 0 <= column + step < cols):
                pairs.append((step, column))
    return pairs


def band_matrix(cols):
    source = np.arange(cols)[:, None]
    target = np.arange(cols)[None, :]
    main = (np.abs(source - target) <= PATCH).astype(np.float32)
    edge = np.zeros((LANES, cols), np.float32)
    for lane, (_, column) in enumerate(edge_pairs(cols)):
        edge[lane] = np.abs(np.arange(cols) - column) <= PATCH
    return np.concatenate([main, main, edge, edge], 0)


def select_matrix(cols):
    pick = np.zeros((LANES, 2 * LANES), np.float32)
    for lane, (step, column) in enumerate(edge_pairs(cols)):
        source = column + 32 if column < 32 else column - cols + 96
        pick[source, lane] = 1.0
        pick[source + step, LANES + lane] = 1.0
    return np.concatenate([pick] * 3, 0)


def keep_masks(cols):
    keep = np.zeros((SPAN, 16, LANES), np.float32)
    for lane, (step, _) in enumerate(edge_pairs(cols)):
        keep[step + SEARCH, :, lane] = 1.0
    return keep


def gain(feature):
    if feature == 2 * CHANS:
        return -6.0
    return 1.0 if feature % CHANS < 3 else 2.0


def partner(feature):
    if feature == 2 * CHANS:
        return feature
    return (feature + CHANS) % (2 * CHANS)


def despeckle(
    sizes, offs_ref, field_ref, band_ref, pick_ref, keep_ref, out_ref,
    above_ref, below_ref, left_ref, right_ref, packs, send_sems, recv_sems,
    feats, moved, own, edges, edge_own, edge_other, edge_dist, edge_sum, dist, sums, weights, totals,
):
    rows, cols, row_total, col_total = sizes
    span_rows = rows + 2 * PAD
    edge_rows = edges.shape[0] // FEATS
    row_tiles = span_rows // 8
    head, tail = PAD // 8, (PAD + rows) // 8
    halves = cols // LANES
    dist_tiles = (rows + 8) // 8
    near_tile, far_tile = 2, dist_tiles - 2
    count = offs_ref.shape[0]
    lane = lax.broadcasted_iota(jnp.int32, (8, LANES), 1)
    sub = lax.broadcasted_iota(jnp.int32, (8, LANES), 0)
    row, col = lax.axis_index("rows"), lax.axis_index("offs")
    row_start, col_start = row * rows, col * cols
    row_count, col_count = lax.axis_size("rows"), lax.axis_size("offs")
    f32, bf16 = jnp.float32, jnp.bfloat16

    def device(down, side):
        return (lax.rem(row + down + row_count, row_count), lax.rem(col + side + col_count, col_count))

    around = [(down, side) for down in (-1, 0, 1) for side in (-1, 0, 1) if (down, side) != (0, 0)]
    barrier = pltpu.get_barrier_semaphore()
    for down, side in around:
        pl.semaphore_signal(barrier, inc=1, device_id=device(down, side), device_id_type=pl.DeviceIdType.MESH)

    def pack(tile, _):
        at = pl.ds(pl.multiple_of(tile * 8, 8), 8)
        first = field_ref[0, at, :LANES]
        last = pltpu.roll(field_ref[0, at, cols - LANES :], RIM, 1)
        for c in range(1, CHANS):
            here = (lane >= RIM * c) & (lane < RIM * (c + 1))
            first = jnp.where(here, pltpu.roll(field_ref[c, at, :LANES], RIM * c, 1), first)
            last = jnp.where(here, pltpu.roll(field_ref[c, at, cols - LANES :], (RIM * c + RIM) % LANES, 1), last)
        packs[0, at, :] = first
        packs[1, at, :] = last
        return 0

    lax.fori_loop(0, rows // 8, pack, 0)

    copies = []
    for k, (down, side) in enumerate(around):
        start, size, put = {-1: (0, PAD, PAD + rows), 0: (0, rows, PAD), 1: (rows - PAD, PAD, 0)}[down]
        if side == 0:
            source = field_ref.at[:, start : start + size, :]
            target = below_ref if down < 0 else above_ref
        else:
            source = packs.at[0 if side < 0 else 1, start : start + size, :]
            target = (right_ref if side < 0 else left_ref).at[put : put + size, :]
        copies.append(pltpu.make_async_remote_copy(
            src_ref=source, dst_ref=target, send_sem=send_sems.at[k], recv_sem=recv_sems.at[k],
            device_id=device(down, side), device_id_type=pl.DeviceIdType.MESH,
        ))

    def features(source_ref, first, groups, tile, _):
        at = pl.ds(pl.multiple_of(tile * 8, 8), 8)
        source_at = pl.ds(pl.multiple_of(tile * 8 - first, 8), 8)
        place = tile * 8 - PAD + sub
        in_rows = (place >= -RIM) & (place < rows + RIM) & (place + row_start >= 0) & (place + row_start < row_total)
        for group in groups:
            column = (group - 1) * LANES + lane
            inside = (
                in_rows & (column >= -RIM) & (column < cols + RIM)
                & (column + col_start >= 0) & (column + col_start < col_total)
            )
            if group == 0:
                packed = left_ref[at, :]
                cells = [pltpu.roll(packed, LANES - RIM - RIM * c, 1) for c in range(CHANS)]
            elif group == halves + 1:
                packed = right_ref[at, :]
                cells = [pltpu.roll(packed, LANES - RIM * c, 1) if c else packed for c in range(CHANS)]
            else:
                cells = [source_ref[c, source_at, (group - 1) * LANES : group * LANES] for c in range(CHANS)]
            adjugate, determinant = hermitian_inverse(cells)
            scale = 1.0 / determinant
            for c in range(CHANS):
                feats[group, c, at, :] = jnp.where(inside, cells[c], 0.0)
                feats[group, CHANS + c, at, :] = jnp.where(inside, adjugate[c] * scale, 0.0)
            feats[group, 2 * CHANS, at, :] = jnp.where(inside, 1.0, 0.0)
        return 0

    def shifts(tile, _):
        at = pl.ds(pl.multiple_of(tile * 8, 8), 8)
        for c in range(FEATS):
            zero = jnp.zeros((8, LANES), f32)
            cells = [zero] + [feats[half + 1, c, at, :] for half in range(halves)] + [zero]
            for step in range(-SEARCH, SEARCH + 1):
                for half in range(halves):
                    here = cells[half + 1]
                    if step > 0:
                        value = pltpu.roll(jnp.where(lane >= step, here, cells[half + 2]), LANES - step, 1)
                    elif step < 0:
                        value = pltpu.roll(jnp.where(lane < LANES + step, here, cells[half]), -step, 1)
                    else:
                        value = here
                    moved[step + SEARCH, half, c, at, :] = value
        return 0

    def own_tiles(tile, _):
        at = pl.ds(pl.multiple_of(tile * 8, 8), 8)
        for half in range(halves):
            for c in range(FEATS):
                own[half, c, at, :] = gain(c) * feats[half + 1, partner(c), pl.ds(tile * 8 + PAD - PATCH, 8), :]
        return 0

    def distances(turn, downs, sides, step, _):
        half, tile = step % halves, step // halves
        at = pl.ds(pl.multiple_of(tile * 8, 8), 8)
        mine = [own[half, c, at, :] for c in range(FEATS)]
        for j in range(BATCH):
            rows_at = pl.ds(tile * 8 + PAD - PATCH + downs[j], 8)
            value = None
            for c in range(FEATS):
                term = mine[c] * moved[sides[j], half, c, rows_at, :]
                value = term if value is None else value + term
            dist[turn * BATCH + j, half, at, :] = value
        return 0

    def distance_batch(spans, turn, _):
        downs = [offs_ref[turn * BATCH + j, 0] for j in range(BATCH)]
        sides = [offs_ref[turn * BATCH + j, 1] + SEARCH for j in range(BATCH)]
        for start, stop in spans:
            lax.fori_loop(start * halves, stop * halves, functools.partial(distances, turn, downs, sides), 0)
        return 0

    inner = tuple(range(1, halves + 1))
    lax.fori_loop(head, tail, functools.partial(features, field_ref, PAD, inner), 0)
    lax.fori_loop(head, tail, shifts, 0)
    lax.fori_loop(near_tile, far_tile, own_tiles, 0)
    pl.semaphore_wait(barrier, len(around))
    for copy in copies:
        copy.start()
    lax.fori_loop(0, count // BATCH, functools.partial(distance_batch, ((near_tile, far_tile),)), 0)
    for copy in copies:
        copy.wait()

    outer = (0, halves + 1)
    lax.fori_loop(0, head, functools.partial(features, above_ref, 0, outer + inner), 0)
    lax.fori_loop(head, tail, functools.partial(features, field_ref, PAD, outer), 0)
    lax.fori_loop(tail, row_tiles, functools.partial(features, below_ref, PAD + rows, outer + inner), 0)
    lax.fori_loop(0, head, shifts, 0)
    lax.fori_loop(tail, row_tiles, shifts, 0)
    lax.fori_loop(0, near_tile, own_tiles, 0)
    lax.fori_loop(far_tile, dist_tiles, own_tiles, 0)
    late = ((0, near_tile), (far_tile, dist_tiles))
    lax.fori_loop(0, count // BATCH, functools.partial(distance_batch, late), 0)

    def split(value):
        high = value.astype(bf16)
        return high, (value - high.astype(f32)).astype(bf16)

    def patches(tile, _):
        at = pl.ds(pl.multiple_of(tile * 8, 8), 8)
        for c in range(FEATS):
            cells = [feats[group, c, at, :] for group in range(halves + 2)]
            before = pltpu.roll(jnp.where(lane >= 96, cells[0], cells[1]), 32, 1)
            after = pltpu.roll(jnp.where(lane >= 96, cells[halves], cells[halves + 1]), 96, 1)
            value = jnp.where(lane < 64, before, after)
            high, rest = value.astype(bf16), value - value.astype(bf16).astype(f32)
            middle, low = split(rest)
            edge_at = pl.ds(pl.multiple_of(c * edge_rows + tile * 8, 8), 8)
            edges[edge_at, :LANES] = high.astype(f32)
            edges[edge_at, LANES : 2 * LANES] = middle.astype(f32)
            edges[edge_at, 2 * LANES :] = low.astype(f32)
            if c < CHANS or c == 2 * CHANS:
                for step in range(1, SEARCH + 1):
                    up, down = (step + SEARCH, halves - 1, c, at), (SEARCH - step, 0, c, at)
                    moved[up] = jnp.where(
                        lane >= LANES - step, pltpu.roll(cells[halves + 1], LANES - step, 1), moved[up]
                    )
                    moved[down] = jnp.where(lane < step, pltpu.roll(cells[0], step, 1), moved[down])
        return 0

    lax.fori_loop(0, row_tiles, patches, 0)

    def edge_pick(c, _):
        at = pl.ds(pl.multiple_of(c * edge_rows, 8), edge_rows)
        both = jnp.dot(edges[at, :].astype(bf16), pick_ref[...], preferred_element_type=f32)
        edge_own[at, :] = both[:, :LANES]
        edge_other[at, :] = both[:, LANES:]
        return 0

    lax.fori_loop(0, FEATS, edge_pick, 0)

    def edge_tiles(tile, _):
        at = pl.ds(pl.multiple_of(tile * 8, 8), 8)
        mine = [
            gain(c) * edge_own[pl.ds(partner(c) * edge_rows + tile * 8 + PAD - PATCH, 8), :]
            for c in range(FEATS)
        ]
        for step in range(SPAN):
            value = None
            for c in range(FEATS):
                rows_at = pl.ds(c * edge_rows + tile * 8 + PAD - PATCH - SEARCH + step, 8)
                term = mine[c] * edge_other[rows_at, :]
                value = term if value is None else value + term
            edge_dist[step, at, :] = value
        return 0

    lax.fori_loop(0, dist_tiles, edge_tiles, 0)

    def edge_sums(step, _):
        for part in range(rows // 16):
            value = edge_dist[step, pl.ds(16 * part, 16), :]
            for s in range(1, SIDE):
                value = value + edge_dist[step, pl.ds(16 * part + s, 16), :]
            high, low = split(value)
            edge_sum[step, 16 * part : 16 * part + 16, :LANES] = high
            edge_sum[step, 16 * part : 16 * part + 16, LANES:] = low
        return 0

    lax.fori_loop(0, SPAN, edge_sums, 0)
    totals[...] = jnp.zeros_like(totals)

    def batch(turn, _):
        downs = [offs_ref[turn * GROUP + j, 0] for j in range(GROUP)]
        sides = [offs_ref[turn * GROUP + j, 1] + SEARCH for j in range(GROUP)]

        def window(j, _):
            k = turn * GROUP + j
            down = offs_ref[k, 0] + SEARCH
            keep = keep_ref[offs_ref[k, 1] + SEARCH]
            for part in range(rows // 16):
                at = pl.ds(pl.multiple_of(j * rows + 16 * part, 16), 16)
                for half in range(halves):
                    value = dist[k, half, pl.ds(16 * part, 16), :]
                    for s in range(1, SIDE):
                        value = value + dist[k, half, pl.ds(16 * part + s, 16), :]
                    high, low = split(value)
                    sums[at, half * LANES : (half + 1) * LANES] = high
                    sums[at, cols + half * LANES : cols + (half + 1) * LANES] = low
                for k2 in range(2):
                    sums[at, 2 * cols + k2 * LANES : 2 * cols + (k2 + 1) * LANES] = (
                        edge_sum[down, 16 * part : 16 * part + 16, k2 * LANES : (k2 + 1) * LANES] * keep
                    )
            return 0

        lax.fori_loop(0, GROUP, window, 0)

        patch = jnp.dot(sums[...], band_ref[...], preferred_element_type=f32)
        weights[...] = jnp.exp2(patch * EXPONENT)

        def accumulate(tile, _):
            at = pl.ds(pl.multiple_of(tile * 8, 8), 8)
            for half in range(halves):
                total = [totals[half, c, at, :] for c in range(CHANS + 1)]
                for j in range(GROUP):
                    rows_at = pl.ds(tile * 8 + PAD + downs[j], 8)
                    weight = weights[
                        pl.ds(pl.multiple_of(j * rows + tile * 8, 8), 8), half * LANES : (half + 1) * LANES
                    ]
                    for c in range(CHANS):
                        total[c] = total[c] + weight * moved[sides[j], half, c, rows_at, :]
                    total[CHANS] = total[CHANS] + weight * moved[sides[j], half, 2 * CHANS, rows_at, :]
                for c in range(CHANS + 1):
                    totals[half, c, at, :] = total[c]
            return 0

        lax.fori_loop(0, rows // 8, accumulate, 0)
        return 0

    lax.fori_loop(0, count // GROUP, batch, 0)

    def finish(tile, _):
        at = pl.ds(pl.multiple_of(tile * 8, 8), 8)
        for half in range(halves):
            span = slice(half * LANES, (half + 1) * LANES)
            scale = 1.0 / (1.0 + totals[half, CHANS, at, :])
            for c in range(CHANS):
                out_ref[c, at, span] = (field_ref[c, at, span] + totals[half, c, at, :]) * scale
        return 0

    lax.fori_loop(0, rows // 8, finish, 0)


def filter_block(sizes, offsets, field):
    rows, cols = sizes[:2]
    span_rows = rows + 2 * PAD
    edge_rows = span_rows + 8
    halves = cols // LANES
    vmem = pl.BlockSpec(memory_space=pltpu.VMEM)
    smem = pl.BlockSpec(memory_space=pltpu.SMEM)
    f32, bf16 = jnp.float32, jnp.bfloat16
    return pl.pallas_call(
        functools.partial(despeckle, sizes),
        out_shape=jax.ShapeDtypeStruct((CHANS, rows, cols), f32),
        in_specs=[smem] + [vmem] * 4,
        out_specs=vmem,
        scratch_shapes=[
            pltpu.VMEM((CHANS, PAD, cols), f32),
            pltpu.VMEM((CHANS, PAD, cols), f32),
            pltpu.VMEM((span_rows, LANES), f32),
            pltpu.VMEM((span_rows, LANES), f32),
            pltpu.VMEM((2, rows, LANES), f32),
            pltpu.SemaphoreType.DMA((8,)),
            pltpu.SemaphoreType.DMA((8,)),
            pltpu.VMEM((halves + 2, FEATS, span_rows + BANKS, LANES), f32),
            pltpu.VMEM((SPAN, halves, FEATS, span_rows + BANKS, LANES), f32),
            pltpu.VMEM((halves, FEATS, rows + BANKS, LANES), f32),
            pltpu.VMEM((FEATS * edge_rows, 3 * LANES), f32),
            pltpu.VMEM((FEATS * edge_rows, LANES), f32),
            pltpu.VMEM((FEATS * edge_rows, LANES), f32),
            pltpu.VMEM((SPAN, rows + 8, LANES), f32),
            pltpu.VMEM((SPAN, rows, 2 * LANES), bf16),
            pltpu.VMEM((offsets.shape[0], halves, rows + 8, LANES), f32),
            pltpu.VMEM((GROUP * rows, 2 * cols + 2 * LANES), bf16),
            pltpu.VMEM((GROUP * rows, cols), f32),
            pltpu.VMEM((halves, CHANS + 1, rows + BANKS, LANES), f32),
        ],
        compiler_params=pltpu.CompilerParams(
            vmem_limit_bytes=62 * 1024 * 1024, collective_id=0, has_side_effects=True
        ),
    )(
        offsets, field, jnp.asarray(band_matrix(cols), bf16), jnp.asarray(select_matrix(cols), bf16),
        jnp.asarray(keep_masks(cols), bf16),
    )


def per_device(coherency_field, offsets):
    _, rows, cols = coherency_field.shape
    row_total = rows * lax.axis_size("rows")
    col_total = cols * lax.axis_size("offs")
    return filter_block((rows, cols, row_total, col_total), offsets, coherency_field)


def solution(mesh):
    in_specs = (P(None, "rows", "offs"), P())
    out_specs = P(None, "rows", "offs")
    return jax.shard_map(
        per_device, mesh=mesh, in_specs=in_specs, out_specs=out_specs, check_vma=False
    )
```

time: 68.1 us -> 60.1 us (0.88)
  Pallas kernels: 64.5 us -> 56.5 us
    pallas_call x1, Pallas kernels: 64.5 us -> 56.5 us  [filter_block(): pl.pallas_call(functools.partial(despeckle, sizes), out_shape=jax.ShapeDt...]
where the time goes in v4:
time: 60.1 us; the launch traced here: 59.9 us
  Pallas kernels  56.5 us (94%)
  local copies, waits for them, and re-layouts  3.32 us (6%)
    pallas_call x1, Pallas kernels, filter_block(): pl.pallas_call(functools.partial(despeckle, sizes), out_shape=jax.ShapeDt...  56.5 us
    unnamed x2, local copies, waits for them, and re-layouts  3.32 us

profile of v4, /device:TPU:1, one launch (start us, length us, event | category | flops | bytes accessed | tf_op | source)
XLA Modules:
  0.0 59.9 jit_solution(7885387584460115123)
XLA Ops:
  0.0 1.4 %copy.6.offs_ref = s32[120,2]{1,0:T(8,128)} copy(s32[120,2]{0,1:T(2,128)} %param.6) | data formatting | bytes 1920 | tf_op args[1]
  1.4 56.5 %shard_map.55 = f32[9,64,256]{2,1,0:T(8,128)} custom-call(s32[120,2]{1,0:T(8,128)} %copy.6.offs_ref, f32[9,64,256]{2,1,0:T(8,128)} %field_ref.1, bf16[768,256]{1,0:T(8,128)(2,1)} %constant.6.clone.band_ref, bf16[384,256]{1,0:T(8,128)(2,1)} %constant.7.clone.pick_ref, bf16[13,16,128]{2,1,0:T(8,128)(2,1)} %constant.8.clone.keep_ref), custom_call_target="tpu_custom_call" | custom-call | tf_op jit(solution)/shard_map/pallas_call | solution.py:396
  58.0 1.9 %copy.8 = f32[9,64,256]{2,1,0:T(8,128)} copy(f32[9,64,256]{2,1,0:T(8,128)} %shard_map.55) | data formatting | bytes 1179648

commit v5 on v4

--- a/solution.py
+++ b/solution.py
@@ -19,8 +19,8 @@
 PAD = 16
 CHANS = 9
 FEATS = 2 * CHANS + 1
-BATCH = 24
-GROUP = 12
+BATCH = 40
+GROUP = 24
 BANKS = 16
 EXPONENT = -math.log2(math.e) / (STRENGTH * SIDE * SIDE)
 
@@ -110,7 +110,7 @@
 def despeckle(
     sizes, offs_ref, field_ref, band_ref, pick_ref, keep_ref, out_ref,
     above_ref, below_ref, left_ref, right_ref, packs, send_sems, recv_sems,
-    feats, moved, own, edges, edge_own, edge_other, edge_dist, edge_sum, dist, sums, weights, totals,
+    feats, moved, own, edges, edge_own, edge_other, edge_dist, edge_sum, dist, sums, weights,
 ):
     rows, cols, row_total, col_total = sizes
     span_rows = rows + 2 * PAD
@@ -120,9 +120,10 @@
     halves = cols // LANES
     dist_tiles = (rows + 8) // 8
     near_tile, far_tile = 2, dist_tiles - 2
-    count = offs_ref.shape[0]
+    count = offs_ref.shape[1]
     lane = lax.broadcasted_iota(jnp.int32, (8, LANES), 1)
     sub = lax.broadcasted_iota(jnp.int32, (8, LANES), 0)
+    wide_lane = lax.broadcasted_iota(jnp.int32, (16, LANES), 1)
     row, col = lax.axis_index("rows"), lax.axis_index("offs")
     row_start, col_start = row * rows, col * cols
     row_count, col_count = lax.axis_size("rows"), lax.axis_size("offs")
@@ -193,8 +194,14 @@
 
     def shifts(tile, _):
         at = pl.ds(pl.multiple_of(tile * 8, 8), 8)
-        for c in range(FEATS):
-            zero = jnp.zeros((8, LANES), f32)
+        zero = jnp.zeros((8, LANES), f32)
+        for step in range(-SEARCH, SEARCH + 1):
+            for half in range(halves):
+                partner_col = half * LANES + lane + step
+                moved[step + SEARCH, half, 2 * CHANS, at, :] = jnp.where(
+                    (partner_col >= 0) & (partner_col < cols), feats[half + 1, 2 * CHANS, at, :], 0.0
+                )
+        for c in range(2 * CHANS):
             cells = [zero] + [feats[half + 1, c, at, :] for half in range(halves)] + [zero]
             for step in range(-SEARCH, SEARCH + 1):
                 for half in range(halves):
@@ -221,27 +228,28 @@
         mine = [own[half, c, at, :] for c in range(FEATS)]
         for j in range(BATCH):
             rows_at = pl.ds(tile * 8 + PAD - PATCH + downs[j], 8)
-            value = None
+            terms = [None, None]
             for c in range(FEATS):
                 term = mine[c] * moved[sides[j], half, c, rows_at, :]
-                value = term if value is None else value + term
-            dist[turn * BATCH + j, half, at, :] = value
+                terms[c % 2] = term if terms[c % 2] is None else terms[c % 2] + term
+            dist[turn * BATCH + j, half, at, :] = terms[0] + terms[1]
         return 0
 
     def distance_batch(spans, turn, _):
-        downs = [offs_ref[turn * BATCH + j, 0] for j in range(BATCH)]
-        sides = [offs_ref[turn * BATCH + j, 1] + SEARCH for j in range(BATCH)]
+        downs = [offs_ref[0, turn * BATCH + j] for j in range(BATCH)]
+        sides = [offs_ref[1, turn * BATCH + j] + SEARCH for j in range(BATCH)]
         for start, stop in spans:
             lax.fori_loop(start * halves, stop * halves, functools.partial(distances, turn, downs, sides), 0)
         return 0
 
     inner = tuple(range(1, halves + 1))
     lax.fori_loop(head, tail, functools.partial(features, field_ref, PAD, inner), 0)
-    lax.fori_loop(head, tail, shifts, 0)
-    lax.fori_loop(near_tile, far_tile, own_tiles, 0)
+    lax.fori_loop(head, tail - 3, shifts, 0)
     pl.semaphore_wait(barrier, len(around))
     for copy in copies:
         copy.start()
+    lax.fori_loop(tail - 3, tail, shifts, 0)
+    lax.fori_loop(near_tile, far_tile, own_tiles, 0)
     lax.fori_loop(0, count // BATCH, functools.partial(distance_batch, ((near_tile, far_tile),)), 0)
     for copy in copies:
         copy.wait()
@@ -262,37 +270,31 @@
         return high, (value - high.astype(f32)).astype(bf16)
 
     def patches(tile, _):
-        at = pl.ds(pl.multiple_of(tile * 8, 8), 8)
+        at = pl.ds(pl.multiple_of(tile * 16, 16), 16)
         for c in range(FEATS):
             cells = [feats[group, c, at, :] for group in range(halves + 2)]
-            before = pltpu.roll(jnp.where(lane >= 96, cells[0], cells[1]), 32, 1)
-            after = pltpu.roll(jnp.where(lane >= 96, cells[halves], cells[halves + 1]), 96, 1)
-            value = jnp.where(lane < 64, before, after)
-            high, rest = value.astype(bf16), value - value.astype(bf16).astype(f32)
-            middle, low = split(rest)
-            edge_at = pl.ds(pl.multiple_of(c * edge_rows + tile * 8, 8), 8)
-            edges[edge_at, :LANES] = high.astype(f32)
-            edges[edge_at, LANES : 2 * LANES] = middle.astype(f32)
-            edges[edge_at, 2 * LANES :] = low.astype(f32)
+            before = pltpu.roll(jnp.where(wide_lane >= 96, cells[0], cells[1]), 32, 1)
+            after = pltpu.roll(jnp.where(wide_lane >= 96, cells[halves], cells[halves + 1]), 96, 1)
+            value = jnp.where(wide_lane < 64, before, after)
+            high = value.astype(bf16)
+            middle, low = split(value - high.astype(f32))
+            edge_at = pl.ds(pl.multiple_of(c * edge_rows + tile * 16, 16), 16)
+            edges[edge_at, :LANES] = high
+            edges[edge_at, LANES : 2 * LANES] = middle
+            edges[edge_at, 2 * LANES :] = low
             if c < CHANS or c == 2 * CHANS:
                 for step in range(1, SEARCH + 1):
                     up, down = (step + SEARCH, halves - 1, c, at), (SEARCH - step, 0, c, at)
                     moved[up] = jnp.where(
-                        lane >= LANES - step, pltpu.roll(cells[halves + 1], LANES - step, 1), moved[up]
+                        wide_lane >= LANES - step, pltpu.roll(cells[halves + 1], LANES - step, 1), moved[up]
                     )
-                    moved[down] = jnp.where(lane < step, pltpu.roll(cells[0], step, 1), moved[down])
-        return 0
-
-    lax.fori_loop(0, row_tiles, patches, 0)
-
-    def edge_pick(c, _):
-        at = pl.ds(pl.multiple_of(c * edge_rows, 8), edge_rows)
-        both = jnp.dot(edges[at, :].astype(bf16), pick_ref[...], preferred_element_type=f32)
-        edge_own[at, :] = both[:, :LANES]
-        edge_other[at, :] = both[:, LANES:]
-        return 0
-
-    lax.fori_loop(0, FEATS, edge_pick, 0)
+                    moved[down] = jnp.where(wide_lane < step, pltpu.roll(cells[0], step, 1), moved[down])
+        return 0
+
+    lax.fori_loop(0, row_tiles // 2, patches, 0)
+    both = jnp.dot(edges[...], pick_ref[...], preferred_element_type=f32)
+    edge_own[...] = both[:, :LANES]
+    edge_other[...] = both[:, LANES:]
 
     def edge_tiles(tile, _):
         at = pl.ds(pl.multiple_of(tile * 8, 8), 8)
@@ -322,80 +324,72 @@
         return 0
 
     lax.fori_loop(0, SPAN, edge_sums, 0)
-    totals[...] = jnp.zeros_like(totals)
-
-    def batch(turn, _):
-        downs = [offs_ref[turn * GROUP + j, 0] for j in range(GROUP)]
-        sides = [offs_ref[turn * GROUP + j, 1] + SEARCH for j in range(GROUP)]
-
-        def window(j, _):
-            k = turn * GROUP + j
-            down = offs_ref[k, 0] + SEARCH
-            keep = keep_ref[offs_ref[k, 1] + SEARCH]
-            for part in range(rows // 16):
-                at = pl.ds(pl.multiple_of(j * rows + 16 * part, 16), 16)
-                for half in range(halves):
-                    value = dist[k, half, pl.ds(16 * part, 16), :]
-                    for s in range(1, SIDE):
-                        value = value + dist[k, half, pl.ds(16 * part + s, 16), :]
-                    high, low = split(value)
-                    sums[at, half * LANES : (half + 1) * LANES] = high
-                    sums[at, cols + half * LANES : cols + (half + 1) * LANES] = low
-                for k2 in range(2):
-                    sums[at, 2 * cols + k2 * LANES : 2 * cols + (k2 + 1) * LANES] = (
-                        edge_sum[down, 16 * part : 16 * part + 16, k2 * LANES : (k2 + 1) * LANES] * keep
-                    )
-            return 0
-
-        lax.fori_loop(0, GROUP, window, 0)
-
-        patch = jnp.dot(sums[...], band_ref[...], preferred_element_type=f32)
-        weights[...] = jnp.exp2(patch * EXPONENT)
-
-        def accumulate(tile, _):
-            at = pl.ds(pl.multiple_of(tile * 8, 8), 8)
+    out_ref[...] = jnp.zeros_like(out_ref)
+    chunk = GROUP * rows // 2
+
+    def window(turn, j, _):
+        k = turn * GROUP + j
+        down = offs_ref[0, k] + SEARCH
+        keep = keep_ref[offs_ref[1, k] + SEARCH]
+        for part in range(rows // 16):
+            at = pl.ds(pl.multiple_of(j * rows + 16 * part, 16), 16)
             for half in range(halves):
-                total = [totals[half, c, at, :] for c in range(CHANS + 1)]
-                for j in range(GROUP):
-                    rows_at = pl.ds(tile * 8 + PAD + downs[j], 8)
-                    weight = weights[
-                        pl.ds(pl.multiple_of(j * rows + tile * 8, 8), 8), half * LANES : (half + 1) * LANES
-                    ]
-                    for c in range(CHANS):
-                        total[c] = total[c] + weight * moved[sides[j], half, c, rows_at, :]
-                    total[CHANS] = total[CHANS] + weight * moved[sides[j], half, 2 * CHANS, rows_at, :]
-                for c in range(CHANS + 1):
-                    totals[half, c, at, :] = total[c]
-            return 0
-
-        lax.fori_loop(0, rows // 8, accumulate, 0)
-        return 0
-
-    lax.fori_loop(0, count // GROUP, batch, 0)
-
-    def finish(tile, _):
+                value = dist[k, half, pl.ds(16 * part, 16), :]
+                for s in range(1, SIDE):
+                    value = value + dist[k, half, pl.ds(16 * part + s, 16), :]
+                high, low = split(value)
+                sums[at, half * LANES : (half + 1) * LANES] = high
+                sums[at, cols + half * LANES : cols + (half + 1) * LANES] = low
+            for which in range(2):
+                span = slice(which * LANES, (which + 1) * LANES)
+                sums[at, 2 * cols + which * LANES : 2 * cols + (which + 1) * LANES] = (
+                    edge_sum[down, 16 * part : 16 * part + 16, span] * keep
+                )
+        return 0
+
+    def weigh(piece, _):
+        at = pl.ds(pl.multiple_of(piece * chunk, chunk), chunk)
+        patch = jnp.dot(sums[at, :], band_ref[...], preferred_element_type=f32)
+        weights[at, :] = jnp.exp2(patch * EXPONENT)
+        return 0
+
+    def accumulate(turn, downs, sides, tile, _):
         at = pl.ds(pl.multiple_of(tile * 8, 8), 8)
         for half in range(halves):
             span = slice(half * LANES, (half + 1) * LANES)
-            scale = 1.0 / (1.0 + totals[half, CHANS, at, :])
-            for c in range(CHANS):
-                out_ref[c, at, span] = (field_ref[c, at, span] + totals[half, c, at, :]) * scale
-        return 0
-
-    lax.fori_loop(0, rows // 8, finish, 0)
+            total = [out_ref[c, at, span] for c in range(CHANS + 1)]
+            for j in range(GROUP):
+                rows_at = pl.ds(tile * 8 + PAD + downs[j], 8)
+                weight = weights[pl.ds(pl.multiple_of(j * rows + tile * 8, 8), 8), span]
+                for c in range(CHANS):
+                    total[c] = total[c] + weight * moved[sides[j], half, c, rows_at, :]
+                total[CHANS] = total[CHANS] + weight * moved[sides[j], half, 2 * CHANS, rows_at, :]
+            for c in range(CHANS + 1):
+                out_ref[c, at, span] = total[c]
+        return 0
+
+    def group(turn, _):
+        downs = [offs_ref[0, turn * GROUP + j] for j in range(GROUP)]
+        sides = [offs_ref[1, turn * GROUP + j] + SEARCH for j in range(GROUP)]
+        lax.fori_loop(0, GROUP, functools.partial(window, turn), 0)
+        lax.fori_loop(0, 2, weigh, 0)
+        lax.fori_loop(0, rows // 8, functools.partial(accumulate, turn, downs, sides), 0)
+        return 0
+
+    lax.fori_loop(0, count // GROUP, group, 0)
 
 
 def filter_block(sizes, offsets, field):
     rows, cols = sizes[:2]
     span_rows = rows + 2 * PAD
-    edge_rows = span_rows + 8
+    edge_rows = span_rows + BANKS
     halves = cols // LANES
     vmem = pl.BlockSpec(memory_space=pltpu.VMEM)
     smem = pl.BlockSpec(memory_space=pltpu.SMEM)
     f32, bf16 = jnp.float32, jnp.bfloat16
     return pl.pallas_call(
         functools.partial(despeckle, sizes),
-        out_shape=jax.ShapeDtypeStruct((CHANS, rows, cols), f32),
+        out_shape=jax.ShapeDtypeStruct((CHANS + 1, rows, cols), f32),
         in_specs=[smem] + [vmem] * 4,
         out_specs=vmem,
         scratch_shapes=[
@@ -409,7 +403,7 @@
             pltpu.VMEM((halves + 2, FEATS, span_rows + BANKS, LANES), f32),
             pltpu.VMEM((SPAN, halves, FEATS, span_rows + BANKS, LANES), f32),
             pltpu.VMEM((halves, FEATS, rows + BANKS, LANES), f32),
-            pltpu.VMEM((FEATS * edge_rows, 3 * LANES), f32),
+            pltpu.VMEM((FEATS * edge_rows, 3 * LANES), bf16),
             pltpu.VMEM((FEATS * edge_rows, LANES), f32),
             pltpu.VMEM((FEATS * edge_rows, LANES), f32),
             pltpu.VMEM((SPAN, rows + 8, LANES), f32),
@@ -417,13 +411,12 @@
             pltpu.VMEM((offsets.shape[0], halves, rows + 8, LANES), f32),
             pltpu.VMEM((GROUP * rows, 2 * cols + 2 * LANES), bf16),
             pltpu.VMEM((GROUP * rows, cols), f32),
-            pltpu.VMEM((halves, CHANS + 1, rows + BANKS, LANES), f32),
         ],
         compiler_params=pltpu.CompilerParams(
             vmem_limit_bytes=62 * 1024 * 1024, collective_id=0, has_side_effects=True
         ),
     )(
-        offsets, field, jnp.asarray(band_matrix(cols), bf16), jnp.asarray(select_matrix(cols), bf16),
+        offsets.T, field, jnp.asarray(band_matrix(cols), bf16), jnp.asarray(select_matrix(cols), bf16),
         jnp.asarray(keep_masks(cols), bf16),
     )
 
@@ -432,7 +425,8 @@
     _, rows, cols = coherency_field.shape
     row_total = rows * lax.axis_size("rows")
     col_total = cols * lax.axis_size("offs")
-    return filter_block((rows, cols, row_total, col_total), offsets, coherency_field)
+    sums = filter_block((rows, cols, row_total, col_total), offsets, coherency_field)
+    return (coherency_field + sums[:CHANS]) / (1.0 + sums[CHANS])
 
 
 def solution(mesh):

time: 60.1 us -> 57.4 us (0.955)
  local copies, waits for them, and re-layouts: 3.32 us -> 0.01 us
  other arithmetic: 0 us -> 2.81 us
  Pallas kernels: 56.5 us -> 54.4 us
    unnamed x2, local copies, waits for them, and re-layouts: 3.32 us -> 0.01 us
    div x0 -> x2, other arithmetic: none -> 2.81 us  [per_device(): return (coherency_field + sums[:CHANS]) / (1.0 + sums[CHANS])]
    pallas_call x1, Pallas kernels: 56.5 us -> 54.4 us  [filter_block(): pl.pallas_call(functools.partial(despeckle, sizes), out_shape=jax.ShapeDt...]
where the time goes in v5:
time: 57.4 us; the launch traced here: 57.2 us
  Pallas kernels  54.4 us (95%)
  other arithmetic  2.81 us (5%)
    pallas_call x1, Pallas kernels, filter_block(): pl.pallas_call(functools.partial(despeckle, sizes), out_shape=jax.ShapeDt...  54.4 us
    div x2, other arithmetic, per_device(): return (coherency_field + sums[:CHANS]) / (1.0 + sums[CHANS])  2.81 us

profile of v5, /device:TPU:1, one launch (start us, length us, event | category | flops | bytes accessed | tf_op | source)
XLA Modules:
  0.0 57.2 jit_solution(10774933558234808694)
XLA Ops:
  0.0 0.0 copy-start
  0.0 54.4 %shard_map.55 = f32[10,64,256]{2,1,0:T(8,128)} custom-call(s32[2,120]{1,0:T(2,128)} %bitcast.3, f32[9,64,256]{2,1,0:T(8,128)} %field_ref.1, bf16[768,256]{1,0:T(8,128)(2,1)} %constant.8.clone.band_ref, bf16[384,256]{1,0:T(8,128)(2,1)} %constant.9.clone.pick_ref, bf16[13,16,128]{2,1,0:T(8,128)(2,1)} %constant.10.clone.keep_ref), custom_call_target="tpu_custom_call" | custom-call | tf_op jit(solution)/shard_map/pallas_call | solution.py:390
  54.4 0.8 %add_bitcast_fusion = f32[64,256]{1,0:T(8,128)S(1)} fusion(f32[10,64,256]{2,1,0:T(8,128)} %shard_map.55), kind=kLoop, calls=%fused_computation.1 | loop fusion | flops 16384 | bytes 131072 | tf_op jit(solution)/shard_map/div | solution.py:429
  55.2 0.0 copy-done
  55.2 2.0 %add_divide_fusion = f32[9,64,256]{2,1,0:T(8,128)} fusion(f32[9,64,256]{2,1,0:T(8,128)S(1)} %copy-done, f32[10,64,256]{2,1,0:T(8,128)} %shard_map.55, f32[64,256]{1,0:T(8,128)S(1)} %add_bitcast_fusion), kind=kLoop, calls=%fused_computation | loop fusion | flops 294912 | bytes 1835008 | tf_op jit(solution)/shard_map/div | solution.py:429
Async XLA Ops:
  0.0 55.2 %copy-start = (f32[9,64,256]{2,1,0:T(8,128)S(1)}, f32[9,64,256]{2,1,0:T(8,128)}, u32[]{:S(2)}) copy-start(f32[9,64,256]{2,1,0:T(8,128)} %field_ref.1) | copy-start | bytes 1769476

commit v6 on v5

--- a/solution.py
+++ b/solution.py
@@ -129,13 +129,19 @@
     row_count, col_count = lax.axis_size("rows"), lax.axis_size("offs")
     f32, bf16 = jnp.float32, jnp.bfloat16
 
-    def device(down, side):
-        return (lax.rem(row + down + row_count, row_count), lax.rem(col + side + col_count, col_count))
+    def present(down, side):
+        return (row + down >= 0) & (row + down < row_count) & (col + side >= 0) & (col + side < col_count)
 
     around = [(down, side) for down in (-1, 0, 1) for side in (-1, 0, 1) if (down, side) != (0, 0)]
     barrier = pltpu.get_barrier_semaphore()
     for down, side in around:
-        pl.semaphore_signal(barrier, inc=1, device_id=device(down, side), device_id_type=pl.DeviceIdType.MESH)
+
+        @pl.when(present(down, side))
+        def _(down=down, side=side):
+            pl.semaphore_signal(
+                barrier, inc=1, device_id=(row + down, col + side), device_id_type=pl.DeviceIdType.MESH
+            )
+
 
     def pack(tile, _):
         at = pl.ds(pl.multiple_of(tile * 8, 8), 8)
@@ -162,7 +168,7 @@
             target = (right_ref if side < 0 else left_ref).at[put : put + size, :]
         copies.append(pltpu.make_async_remote_copy(
             src_ref=source, dst_ref=target, send_sem=send_sems.at[k], recv_sem=recv_sems.at[k],
-            device_id=device(down, side), device_id_type=pl.DeviceIdType.MESH,
+            device_id=(row + down, col + side), device_id_type=pl.DeviceIdType.MESH,
         ))
 
     def features(source_ref, first, groups, tile, _):
@@ -244,15 +250,18 @@
 
     inner = tuple(range(1, halves + 1))
     lax.fori_loop(head, tail, functools.partial(features, field_ref, PAD, inner), 0)
-    lax.fori_loop(head, tail - 3, shifts, 0)
-    pl.semaphore_wait(barrier, len(around))
-    for copy in copies:
-        copy.start()
-    lax.fori_loop(tail - 3, tail, shifts, 0)
+    lax.fori_loop(head, tail - 1, shifts, 0)
+    over = 1 + (row > 0).astype(jnp.int32) + (row < row_count - 1).astype(jnp.int32)
+    across = 1 + (col > 0).astype(jnp.int32) + (col < col_count - 1).astype(jnp.int32)
+    pl.semaphore_wait(barrier, over * across - 1)
+    for (down, side), copy in zip(around, copies):
+        pl.when(present(down, side))(copy.start)
+    lax.fori_loop(tail - 1, tail, shifts, 0)
     lax.fori_loop(near_tile, far_tile, own_tiles, 0)
     lax.fori_loop(0, count // BATCH, functools.partial(distance_batch, ((near_tile, far_tile),)), 0)
-    for copy in copies:
-        copy.wait()
+    for (down, side), copy in zip(around, copies):
+        pl.when(present(down, side))(copy.wait_send)
+        pl.when(present(-down, -side))(copy.wait_recv)
 
     outer = (0, halves + 1)
     lax.fori_loop(0, head, functools.partial(features, above_ref, 0, outer + inner), 0)
@@ -377,6 +386,17 @@
         return 0
 
     lax.fori_loop(0, count // GROUP, group, 0)
+
+
+def finish(field_ref, sums_ref, out_ref):
+    def tile_rows(tile, _):
+        at = pl.ds(pl.multiple_of(tile * 8, 8), 8)
+        scale = 1.0 / (1.0 + sums_ref[CHANS, at, :])
+        for c in range(CHANS):
+            out_ref[c, at, :] = (field_ref[c, at, :] + sums_ref[c, at, :]) * scale
+        return 0
+
+    lax.fori_loop(0, field_ref.shape[1] // 8, tile_rows, 0)
 
 
 def filter_block(sizes, offsets, field):
@@ -426,7 +446,13 @@
     row_total = rows * lax.axis_size("rows")
     col_total = cols * lax.axis_size("offs")
     sums = filter_block((rows, cols, row_total, col_total), offsets, coherency_field)
-    return (coherency_field + sums[:CHANS]) / (1.0 + sums[CHANS])
+    vmem = pl.BlockSpec(memory_space=pltpu.VMEM)
+    return pl.pallas_call(
+        finish,
+        out_shape=jax.ShapeDtypeStruct(coherency_field.shape, jnp.float32),
+        in_specs=[vmem, vmem],
+        out_specs=vmem,
+    )(coherency_field, sums)
 
 
 def solution(mesh):

time: 57.4 us -> 53.9 us (0.939)
  the two profiles are of different devices: /device:TPU:1 before, /device:TPU:3 now
where the time goes in v6:
time: 53.9 us; the launch traced here: 53.8 us
  Pallas kernels  53.8 us (100%)
    pallas_call x1, Pallas kernels, filter_block(): pl.pallas_call(functools.partial(despeckle, sizes), out_shape=jax.ShapeDt...  51.6 us
    pallas_call x1, Pallas kernels, per_device(): pl.pallas_call(finish, out_shape=jax.ShapeDtypeStruct(coherency_field.sha...  2.2 us

profile of v6, /device:TPU:3, one launch (start us, length us, event | category | flops | bytes accessed | tf_op | source)
XLA Modules:
  0.0 53.8 jit_solution(16289776542453965645)
XLA Ops:
  0.0 51.6 %shard_map.55.sums_ref = f32[10,64,256]{2,1,0:T(8,128)} custom-call(s32[2,120]{1,0:T(2,128)} %bitcast.1, f32[9,64,256]{2,1,0:T(8,128)} %field_ref.3, bf16[768,256]{1,0:T(8,128)(2,1)} %constant.6.clone.band_ref, bf16[384,256]{1,0:T(8,128)(2,1)} %constant.7.clone.pick_ref, bf16[13,16,128]{2,1,0:T(8,128)(2,1)} %constant.8.clone.keep_ref), custom_call_target="tpu_custom_call" | custom-call | tf_op jit(solution)/shard_map/pallas_call | solution.py:410
  51.6 2.2 %shard_map.56 = f32[9,64,256]{2,1,0:T(8,128)} custom-call(f32[9,64,256]{2,1,0:T(8,128)} %field_ref.3, f32[10,64,256]{2,1,0:T(8,128)} %shard_map.55.sums_ref), custom_call_target="tpu_custom_call" | custom-call | tf_op jit(solution)/shard_map/pallas_call | solution.py:450

commit v7 on v6

--- a/solution.py
+++ b/solution.py
@@ -20,6 +20,7 @@
 CHANS = 9
 FEATS = 2 * CHANS + 1
 BATCH = 40
+AHEAD = 1
 GROUP = 24
 BANKS = 16
 EXPONENT = -math.log2(math.e) / (STRENGTH * SIDE * SIDE)
@@ -250,35 +251,45 @@
 
     inner = tuple(range(1, halves + 1))
     lax.fori_loop(head, tail, functools.partial(features, field_ref, PAD, inner), 0)
-    lax.fori_loop(head, tail - 1, shifts, 0)
+    def distance_span(first_batch, last_batch, start, stop):
+        span = functools.partial(distance_batch, ((start, stop),))
+        lax.fori_loop(first_batch, last_batch, span, 0)
+
+    lax.fori_loop(head, tail, shifts, 0)
+    lax.fori_loop(near_tile, far_tile, own_tiles, 0)
+    distance_span(0, AHEAD, near_tile, far_tile)
     over = 1 + (row > 0).astype(jnp.int32) + (row < row_count - 1).astype(jnp.int32)
     across = 1 + (col > 0).astype(jnp.int32) + (col < col_count - 1).astype(jnp.int32)
     pl.semaphore_wait(barrier, over * across - 1)
     for (down, side), copy in zip(around, copies):
         pl.when(present(down, side))(copy.start)
-    lax.fori_loop(tail - 1, tail, shifts, 0)
-    lax.fori_loop(near_tile, far_tile, own_tiles, 0)
-    lax.fori_loop(0, count // BATCH, functools.partial(distance_batch, ((near_tile, far_tile),)), 0)
+    distance_span(AHEAD, count // BATCH, near_tile, far_tile)
+
+    for (down, side), copy in zip(around, copies):
+        if (down, side) == (-1, 0):
+            pl.when(present(-down, -side))(copy.wait_recv)
+    lax.fori_loop(tail, row_tiles, functools.partial(features, below_ref, PAD + rows, inner), 0)
+    lax.fori_loop(tail, row_tiles, shifts, 0)
+    lax.fori_loop(far_tile, dist_tiles, own_tiles, 0)
+    distance_span(0, count // BATCH, far_tile, dist_tiles)
+
     for (down, side), copy in zip(around, copies):
         pl.when(present(down, side))(copy.wait_send)
-        pl.when(present(-down, -side))(copy.wait_recv)
-
+        if (down, side) != (-1, 0):
+            pl.when(present(-down, -side))(copy.wait_recv)
     outer = (0, halves + 1)
     lax.fori_loop(0, head, functools.partial(features, above_ref, 0, outer + inner), 0)
     lax.fori_loop(head, tail, functools.partial(features, field_ref, PAD, outer), 0)
-    lax.fori_loop(tail, row_tiles, functools.partial(features, below_ref, PAD + rows, outer + inner), 0)
+    lax.fori_loop(tail, row_tiles, functools.partial(features, below_ref, PAD + rows, outer), 0)
     lax.fori_loop(0, head, shifts, 0)
-    lax.fori_loop(tail, row_tiles, shifts, 0)
     lax.fori_loop(0, near_tile, own_tiles, 0)
-    lax.fori_loop(far_tile, dist_tiles, own_tiles, 0)
-    late = ((0, near_tile), (far_tile, dist_tiles))
-    lax.fori_loop(0, count // BATCH, functools.partial(distance_batch, late), 0)
+    distance_span(0, count // BATCH, 0, near_tile)
 
     def split(value):
         high = value.astype(bf16)
         return high, (value - high.astype(f32)).astype(bf16)
 
-    def patches(tile, _):
+    def edge_columns(tile, _):
         at = pl.ds(pl.multiple_of(tile * 16, 16), 16)
         for c in range(FEATS):
             cells = [feats[group, c, at, :] for group in range(halves + 2)]
@@ -291,16 +302,27 @@
             edges[edge_at, :LANES] = high
             edges[edge_at, LANES : 2 * LANES] = middle
             edges[edge_at, 2 * LANES :] = low
-            if c < CHANS or c == 2 * CHANS:
-                for step in range(1, SEARCH + 1):
-                    up, down = (step + SEARCH, halves - 1, c, at), (SEARCH - step, 0, c, at)
-                    moved[up] = jnp.where(
-                        wide_lane >= LANES - step, pltpu.roll(cells[halves + 1], LANES - step, 1), moved[up]
-                    )
-                    moved[down] = jnp.where(wide_lane < step, pltpu.roll(cells[0], step, 1), moved[down])
-        return 0
-
-    lax.fori_loop(0, row_tiles // 2, patches, 0)
+        return 0
+
+    def patches(tile, _):
+        at = pl.ds(pl.multiple_of(tile * 8, 8), 8)
+        valid = feats[1, 2 * CHANS, at, :]
+        for step in range(1, SEARCH + 1):
+            for move, half in ((step, halves - 1), (-step, 0)):
+                column = col_start + half * LANES + lane + move
+                moved[move + SEARCH, half, 2 * CHANS, at, :] = jnp.where(
+                    (column >= 0) & (column < col_total), valid, 0.0
+                )
+        for c in range(CHANS):
+            before, after = feats[0, c, at, :], feats[halves + 1, c, at, :]
+            for step in range(1, SEARCH + 1):
+                up, down = (step + SEARCH, halves - 1, c, at), (SEARCH - step, 0, c, at)
+                moved[up] = jnp.where(lane >= LANES - step, pltpu.roll(after, LANES - step, 1), moved[up])
+                moved[down] = jnp.where(lane < step, pltpu.roll(before, step, 1), moved[down])
+        return 0
+
+    lax.fori_loop(1, row_tiles - 1, patches, 0)
+    lax.fori_loop(0, row_tiles // 2, edge_columns, 0)
     both = jnp.dot(edges[...], pick_ref[...], preferred_element_type=f32)
     edge_own[...] = both[:, :LANES]
     edge_other[...] = both[:, LANES:]

time: 53.9 us -> 53 us (0.983)
  the two profiles are of different devices: /device:TPU:3 before, /device:TPU:1 now
where the time goes in v7:
time: 53 us; the launch traced here: 52.4 us
  Pallas kernels  52.4 us (99%)
    pallas_call x1, Pallas kernels, filter_block(): pl.pallas_call(functools.partial(despeckle, sizes), out_shape=jax.ShapeDt...  50.2 us
    pallas_call x1, Pallas kernels, per_device(): pl.pallas_call(finish, out_shape=jax.ShapeDtypeStruct(coherency_field.sha...  2.2 us

profile of v7, /device:TPU:1, one launch (start us, length us, event | category | flops | bytes accessed | tf_op | source)
XLA Modules:
  0.0 52.4 jit_solution(2850458209083051570)
XLA Ops:
  0.0 50.2 %shard_map.55.sums_ref = f32[10,64,256]{2,1,0:T(8,128)} custom-call(s32[2,120]{1,0:T(2,128)} %bitcast.1, f32[9,64,256]{2,1,0:T(8,128)} %field_ref.3, bf16[768,256]{1,0:T(8,128)(2,1)} %constant.6.clone.band_ref, bf16[384,256]{1,0:T(8,128)(2,1)} %constant.7.clone.pick_ref, bf16[13,16,128]{2,1,0:T(8,128)(2,1)} %constant.8.clone.keep_ref), custom_call_target="tpu_custom_call" | custom-call | tf_op jit(solution)/shard_map/pallas_call | solution.py:432
  50.2 2.2 %shard_map.56 = f32[9,64,256]{2,1,0:T(8,128)} custom-call(f32[9,64,256]{2,1,0:T(8,128)} %field_ref.3, f32[10,64,256]{2,1,0:T(8,128)} %shard_map.55.sums_ref), custom_call_target="tpu_custom_call" | custom-call | tf_op jit(solution)/shard_map/pallas_call | solution.py:472

commit v8 on v7

--- a/solution.py
+++ b/solution.py
@@ -21,7 +21,9 @@
 FEATS = 2 * CHANS + 1
 BATCH = 40
 AHEAD = 1
-GROUP = 24
+GROUP = 40
+FAR = 1e30
+SPARE = 120
 BANKS = 16
 EXPONENT = -math.log2(math.e) / (STRENGTH * SIDE * SIDE)
 
@@ -77,7 +79,12 @@
     edge = np.zeros((LANES, cols), np.float32)
     for lane, (_, column) in enumerate(edge_pairs(cols)):
         edge[lane] = np.abs(np.arange(cols) - column) <= PATCH
-    return np.concatenate([main, main, edge, edge], 0)
+    high, low = edge.copy(), edge.copy()
+    for place in range(SEARCH):
+        high[SPARE + place, place] = 1.0
+        low[SPARE + place, cols - SEARCH + place] = 1.0
+    high[SPARE + SEARCH] = 1.0
+    return np.concatenate([main, main, high, low], 0)
 
 
 def select_matrix(cols):
@@ -111,7 +118,7 @@
 def despeckle(
     sizes, offs_ref, field_ref, band_ref, pick_ref, keep_ref, out_ref,
     above_ref, below_ref, left_ref, right_ref, packs, send_sems, recv_sems,
-    feats, moved, own, edges, edge_own, edge_other, edge_dist, edge_sum, dist, sums, weights,
+    feats, moved, own, edges, edge_own, edge_other, edge_dist, edge_sum, dist, sums, weights, keeps,
 ):
     rows, cols, row_total, col_total = sizes
     span_rows = rows + 2 * PAD
@@ -124,6 +131,7 @@
     count = offs_ref.shape[1]
     lane = lax.broadcasted_iota(jnp.int32, (8, LANES), 1)
     sub = lax.broadcasted_iota(jnp.int32, (8, LANES), 0)
+    wide_sub = lax.broadcasted_iota(jnp.int32, (16, LANES), 0)
     wide_lane = lax.broadcasted_iota(jnp.int32, (16, LANES), 1)
     row, col = lax.axis_index("rows"), lax.axis_index("offs")
     row_start, col_start = row * rows, col * cols
@@ -306,13 +314,6 @@
 
     def patches(tile, _):
         at = pl.ds(pl.multiple_of(tile * 8, 8), 8)
-        valid = feats[1, 2 * CHANS, at, :]
-        for step in range(1, SEARCH + 1):
-            for move, half in ((step, halves - 1), (-step, 0)):
-                column = col_start + half * LANES + lane + move
-                moved[move + SEARCH, half, 2 * CHANS, at, :] = jnp.where(
-                    (column >= 0) & (column < col_total), valid, 0.0
-                )
         for c in range(CHANS):
             before, after = feats[0, c, at, :], feats[halves + 1, c, at, :]
             for step in range(1, SEARCH + 1):
@@ -321,7 +322,6 @@
                 moved[down] = jnp.where(lane < step, pltpu.roll(before, step, 1), moved[down])
         return 0
 
-    lax.fori_loop(1, row_tiles - 1, patches, 0)
     lax.fori_loop(0, row_tiles // 2, edge_columns, 0)
     both = jnp.dot(edges[...], pick_ref[...], preferred_element_type=f32)
     edge_own[...] = both[:, :LANES]
@@ -349,19 +349,38 @@
             value = edge_dist[step, pl.ds(16 * part, 16), :]
             for s in range(1, SIDE):
                 value = value + edge_dist[step, pl.ds(16 * part + s, 16), :]
-            high, low = split(value)
+            partner_row = row_start + 16 * part + wide_sub + step - SEARCH
+            outside = (partner_row < 0) | (partner_row >= row_total)
+            high, low = split(jnp.where(wide_lane >= SPARE, 0.0, value))
+            far = jnp.where((wide_lane < SPARE + SEARCH) | outside, FAR, 0.0)
+            high = jnp.where(wide_lane >= SPARE, far, high.astype(f32)).astype(bf16)
+            low = jnp.where(wide_lane >= SPARE, FAR, low.astype(f32)).astype(bf16)
             edge_sum[step, 16 * part : 16 * part + 16, :LANES] = high
             edge_sum[step, 16 * part : 16 * part + 16, LANES:] = low
         return 0
 
     lax.fori_loop(0, SPAN, edge_sums, 0)
+
+    def keep_tables(step, _):
+        place = wide_lane - SPARE
+        known = keep_ref[step].astype(f32)
+        before = col_start + place + step - SEARCH < 0
+        after = col_start + cols - SEARCH + place + step - SEARCH >= col_total
+        spare = (place >= 0) & (place < SEARCH)
+        high = jnp.where((spare & before) | (place == SEARCH), 1.0, known)
+        low = jnp.where(spare & after, 1.0, known)
+        keeps[step, :, :LANES] = high.astype(bf16)
+        keeps[step, :, LANES:] = low.astype(bf16)
+        return 0
+
+    lax.fori_loop(0, SPAN, keep_tables, 0)
     out_ref[...] = jnp.zeros_like(out_ref)
     chunk = GROUP * rows // 2
 
     def window(turn, j, _):
         k = turn * GROUP + j
         down = offs_ref[0, k] + SEARCH
-        keep = keep_ref[offs_ref[1, k] + SEARCH]
+        keep = keeps[offs_ref[1, k] + SEARCH]
         for part in range(rows // 16):
             at = pl.ds(pl.multiple_of(j * rows + 16 * part, 16), 16)
             for half in range(halves):
@@ -374,7 +393,7 @@
             for which in range(2):
                 span = slice(which * LANES, (which + 1) * LANES)
                 sums[at, 2 * cols + which * LANES : 2 * cols + (which + 1) * LANES] = (
-                    edge_sum[down, 16 * part : 16 * part + 16, span] * keep
+                    edge_sum[down, 16 * part : 16 * part + 16, span] * keep[:, span]
                 )
         return 0
 
@@ -394,20 +413,34 @@
                 weight = weights[pl.ds(pl.multiple_of(j * rows + tile * 8, 8), 8), span]
                 for c in range(CHANS):
                     total[c] = total[c] + weight * moved[sides[j], half, c, rows_at, :]
-                total[CHANS] = total[CHANS] + weight * moved[sides[j], half, 2 * CHANS, rows_at, :]
+                total[CHANS] = total[CHANS] + weight
             for c in range(CHANS + 1):
                 out_ref[c, at, span] = total[c]
         return 0
 
-    def group(turn, _):
+    def weigh_and_add(turn):
         downs = [offs_ref[0, turn * GROUP + j] for j in range(GROUP)]
         sides = [offs_ref[1, turn * GROUP + j] + SEARCH for j in range(GROUP)]
-        lax.fori_loop(0, GROUP, functools.partial(window, turn), 0)
         lax.fori_loop(0, 2, weigh, 0)
         lax.fori_loop(0, rows // 8, functools.partial(accumulate, turn, downs, sides), 0)
-        return 0
-
-    lax.fori_loop(0, count // GROUP, group, 0)
+
+    def group(turn, _):
+        lax.fori_loop(0, GROUP, functools.partial(window, turn), 0)
+        weigh_and_add(turn)
+        return 0
+
+    pace = GROUP // (row_tiles - 2)
+
+    def first_group(tile, _):
+        patches(tile, 0)
+        for j in range(pace):
+            window(0, (tile - 1) * pace + j, 0)
+        return 0
+
+    lax.fori_loop(1, row_tiles - 1, first_group, 0)
+    lax.fori_loop(pace * (row_tiles - 2), GROUP, functools.partial(window, 0), 0)
+    weigh_and_add(0)
+    lax.fori_loop(1, count // GROUP, group, 0)
 
 
 def finish(field_ref, sums_ref, out_ref):
@@ -453,6 +486,7 @@
             pltpu.VMEM((offsets.shape[0], halves, rows + 8, LANES), f32),
             pltpu.VMEM((GROUP * rows, 2 * cols + 2 * LANES), bf16),
             pltpu.VMEM((GROUP * rows, cols), f32),
+            pltpu.VMEM((SPAN, 16, 2 * LANES), bf16),
         ],
         compiler_params=pltpu.CompilerParams(
             vmem_limit_bytes=62 * 1024 * 1024, collective_id=0, has_side_effects=True

time: 53 us -> 51.6 us (0.974)
  Pallas kernels: 52.4 us -> 51 us
    pallas_call x1, Pallas kernels: 50.2 us -> 48.8 us  [filter_block(): pl.pallas_call(functools.partial(despeckle, sizes), out_shape=jax.ShapeDt...]
where the time goes in v8:
time: 51.6 us; the launch traced here: 51 us
  Pallas kernels  51 us (99%)
    pallas_call x1, Pallas kernels, filter_block(): pl.pallas_call(functools.partial(despeckle, sizes), out_shape=jax.ShapeDt...  48.8 us
    pallas_call x1, Pallas kernels, per_device(): pl.pallas_call(finish, out_shape=jax.ShapeDtypeStruct(coherency_field.sha...  2.2 us

profile of v8, /device:TPU:1, one launch (start us, length us, event | category | flops | bytes accessed | tf_op | source)
XLA Modules:
  0.0 51.0 jit_solution(8099970600278682297)
XLA Ops:
  0.0 48.8 %shard_map.55.sums_ref = f32[10,64,256]{2,1,0:T(8,128)} custom-call(s32[2,120]{1,0:T(2,128)} %bitcast.1, f32[9,64,256]{2,1,0:T(8,128)} %field_ref.3, bf16[768,256]{1,0:T(8,128)(2,1)} %constant.6.clone.band_ref, bf16[384,256]{1,0:T(8,128)(2,1)} %constant.7.clone.pick_ref, bf16[13,16,128]{2,1,0:T(8,128)(2,1)} %constant.8.clone.keep_ref), custom_call_target="tpu_custom_call" | custom-call | tf_op jit(solution)/shard_map/pallas_call | solution.py:465
  48.8 2.2 %shard_map.56 = f32[9,64,256]{2,1,0:T(8,128)} custom-call(f32[9,64,256]{2,1,0:T(8,128)} %field_ref.3, f32[10,64,256]{2,1,0:T(8,128)} %shard_map.55.sums_ref), custom_call_target="tpu_custom_call" | custom-call | tf_op jit(solution)/shard_map/pallas_call | solution.py:506

commit v9 on v8

--- a/solution.py
+++ b/solution.py
@@ -20,9 +20,9 @@
 CHANS = 9
 FEATS = 2 * CHANS + 1
 BATCH = 40
-AHEAD = 1
+AHEAD = 2
 GROUP = 40
-FAR = 1e30
+FAR = -1e30
 SPARE = 120
 BANKS = 16
 EXPONENT = -math.log2(math.e) / (STRENGTH * SIDE * SIDE)
@@ -105,8 +105,8 @@
 
 def gain(feature):
     if feature == 2 * CHANS:
-        return -6.0
-    return 1.0 if feature % CHANS < 3 else 2.0
+        return -6.0 * EXPONENT
+    return (1.0 if feature % CHANS < 3 else 2.0) * EXPONENT
 
 
 def partner(feature):
@@ -207,27 +207,33 @@
             feats[group, 2 * CHANS, at, :] = jnp.where(inside, 1.0, 0.0)
         return 0
 
-    def shifts(tile, _):
-        at = pl.ds(pl.multiple_of(tile * 8, 8), 8)
-        zero = jnp.zeros((8, LANES), f32)
+    def shift_validity(tile, _):
+        at = pl.ds(pl.multiple_of(tile * 8, 8), 8)
         for step in range(-SEARCH, SEARCH + 1):
             for half in range(halves):
                 partner_col = half * LANES + lane + step
                 moved[step + SEARCH, half, 2 * CHANS, at, :] = jnp.where(
                     (partner_col >= 0) & (partner_col < cols), feats[half + 1, 2 * CHANS, at, :], 0.0
                 )
+        return 0
+
+    def shift_piece(tile, c, step, half):
+        at = pl.ds(pl.multiple_of(tile * 8, 8), 8)
+        value = feats[half + 1, c, at, :]
+        if step:
+            beyond = half + (1 if step > 0 else -1)
+            other = feats[beyond + 1, c, at, :] if 0 <= beyond < halves else jnp.zeros((8, LANES), f32)
+            own_lanes = lane >= step if step > 0 else lane < LANES + step
+            value = pltpu.roll(jnp.where(own_lanes, value, other), (LANES - step) % LANES, 1)
+        moved[step + SEARCH, half, c, at, :] = value
+
+    pieces = [(step, half) for step in range(-SEARCH, SEARCH + 1) for half in range(halves)]
+
+    def shifts(tile, _):
+        shift_validity(tile, 0)
         for c in range(2 * CHANS):
-            cells = [zero] + [feats[half + 1, c, at, :] for half in range(halves)] + [zero]
-            for step in range(-SEARCH, SEARCH + 1):
-                for half in range(halves):
-                    here = cells[half + 1]
-                    if step > 0:
-                        value = pltpu.roll(jnp.where(lane >= step, here, cells[half + 2]), LANES - step, 1)
-                    elif step < 0:
-                        value = pltpu.roll(jnp.where(lane < LANES + step, here, cells[half]), -step, 1)
-                    else:
-                        value = here
-                    moved[step + SEARCH, half, c, at, :] = value
+            for step, half in pieces:
+                shift_piece(tile, c, step, half)
         return 0
 
     def own_tiles(tile, _):
@@ -237,7 +243,7 @@
                 own[half, c, at, :] = gain(c) * feats[half + 1, partner(c), pl.ds(tile * 8 + PAD - PATCH, 8), :]
         return 0
 
-    def distances(turn, downs, sides, step, _):
+    def distances(turn, downs, sides, beside, step, _):
         half, tile = step % halves, step // halves
         at = pl.ds(pl.multiple_of(tile * 8, 8), 8)
         mine = [own[half, c, at, :] for c in range(FEATS)]
@@ -248,13 +254,15 @@
                 term = mine[c] * moved[sides[j], half, c, rows_at, :]
                 terms[c % 2] = term if terms[c % 2] is None else terms[c % 2] + term
             dist[turn * BATCH + j, half, at, :] = terms[0] + terms[1]
+            for piece in beside[j::BATCH]:
+                piece()
         return 0
 
     def distance_batch(spans, turn, _):
         downs = [offs_ref[0, turn * BATCH + j] for j in range(BATCH)]
         sides = [offs_ref[1, turn * BATCH + j] + SEARCH for j in range(BATCH)]
         for start, stop in spans:
-            lax.fori_loop(start * halves, stop * halves, functools.partial(distances, turn, downs, sides), 0)
+            lax.fori_loop(start * halves, stop * halves, functools.partial(distances, turn, downs, sides, ()), 0)
         return 0
 
     inner = tuple(range(1, halves + 1))
@@ -263,15 +271,34 @@
         span = functools.partial(distance_batch, ((start, stop),))
         lax.fori_loop(first_batch, last_batch, span, 0)
 
-    lax.fori_loop(head, tail, shifts, 0)
+    parts = halves * (count // BATCH)
+    share = 2 * CHANS // parts
+    reach = 4
+
+    def inner_distances(shifting, index, _):
+        tile, part = index // parts, index % parts
+        half, turn = part % halves, part // halves
+        downs = [offs_ref[0, turn * BATCH + j] for j in range(BATCH)]
+        sides = [offs_ref[1, turn * BATCH + j] + SEARCH for j in range(BATCH)]
+        beside = []
+        if shifting:
+            for k in range(share):
+                for step, place in pieces:
+                    beside.append(functools.partial(shift_piece, tile + reach, part * share + k, step, place))
+        return distances(turn, downs, sides, beside, tile * halves + half, 0)
+
+    lax.fori_loop(head, head + reach, shifts, 0)
+    lax.fori_loop(head + reach, tail, shift_validity, 0)
     lax.fori_loop(near_tile, far_tile, own_tiles, 0)
-    distance_span(0, AHEAD, near_tile, far_tile)
+    early, full = (near_tile + AHEAD) * parts, (tail - reach) * parts
+    lax.fori_loop(near_tile * parts, early, functools.partial(inner_distances, True), 0)
     over = 1 + (row > 0).astype(jnp.int32) + (row < row_count - 1).astype(jnp.int32)
     across = 1 + (col > 0).astype(jnp.int32) + (col < col_count - 1).astype(jnp.int32)
     pl.semaphore_wait(barrier, over * across - 1)
     for (down, side), copy in zip(around, copies):
         pl.when(present(down, side))(copy.start)
-    distance_span(AHEAD, count // BATCH, near_tile, far_tile)
+    lax.fori_loop(early, full, functools.partial(inner_distances, True), 0)
+    lax.fori_loop(full, far_tile * parts, functools.partial(inner_distances, False), 0)
 
     for (down, side), copy in zip(around, copies):
         if (down, side) == (-1, 0):
@@ -400,7 +427,7 @@
     def weigh(piece, _):
         at = pl.ds(pl.multiple_of(piece * chunk, chunk), chunk)
         patch = jnp.dot(sums[at, :], band_ref[...], preferred_element_type=f32)
-        weights[at, :] = jnp.exp2(patch * EXPONENT)
+        weights[at, :] = jnp.exp2(patch)
         return 0
 
     def accumulate(turn, downs, sides, tile, _):

time: 51.6 us -> 52.5 us (1.017)
  Pallas kernels: 51 us -> 52.3 us
    pallas_call x1, Pallas kernels: 48.8 us -> 50.1 us  [filter_block(): pl.pallas_call(functools.partial(despeckle, sizes), out_shape=jax.ShapeDt...]
where the time goes in v9:
time: 52.5 us; the launch traced here: 52.3 us
  Pallas kernels  52.3 us (100%)
    pallas_call x1, Pallas kernels, filter_block(): pl.pallas_call(functools.partial(despeckle, sizes), out_shape=jax.ShapeDt...  50.1 us
    pallas_call x1, Pallas kernels, per_device(): pl.pallas_call(finish, out_shape=jax.ShapeDtypeStruct(coherency_field.sha...  2.2 us

profile of v9, /device:TPU:1, one launch (start us, length us, event | category | flops | bytes accessed | tf_op | source)
XLA Modules:
  0.0 52.3 jit_solution(7794264792609047042)
XLA Ops:
  0.0 50.1 %shard_map.55.sums_ref = f32[10,64,256]{2,1,0:T(8,128)} custom-call(s32[2,120]{1,0:T(2,128)} %bitcast.1, f32[9,64,256]{2,1,0:T(8,128)} %field_ref.3, bf16[768,256]{1,0:T(8,128)(2,1)} %constant.6.clone.band_ref, bf16[384,256]{1,0:T(8,128)(2,1)} %constant.7.clone.pick_ref, bf16[13,16,128]{2,1,0:T(8,128)(2,1)} %constant.8.clone.keep_ref), custom_call_target="tpu_custom_call" | custom-call | tf_op jit(solution)/shard_map/pallas_call | solution.py:492
  50.1 2.2 %shard_map.56 = f32[9,64,256]{2,1,0:T(8,128)} custom-call(f32[9,64,256]{2,1,0:T(8,128)} %field_ref.3, f32[10,64,256]{2,1,0:T(8,128)} %shard_map.55.sums_ref), custom_call_target="tpu_custom_call" | custom-call | tf_op jit(solution)/shard_map/pallas_call | solution.py:533

commit v10 on v8

--- a/solution.py
+++ b/solution.py
@@ -22,7 +22,7 @@
 BATCH = 40
 AHEAD = 1
 GROUP = 40
-FAR = 1e30
+FAR = -1e30
 SPARE = 120
 BANKS = 16
 EXPONENT = -math.log2(math.e) / (STRENGTH * SIDE * SIDE)
@@ -105,8 +105,8 @@
 
 def gain(feature):
     if feature == 2 * CHANS:
-        return -6.0
-    return 1.0 if feature % CHANS < 3 else 2.0
+        return -6.0 * EXPONENT
+    return (1.0 if feature % CHANS < 3 else 2.0) * EXPONENT
 
 
 def partner(feature):
@@ -265,12 +265,13 @@
 
     lax.fori_loop(head, tail, shifts, 0)
     lax.fori_loop(near_tile, far_tile, own_tiles, 0)
-    distance_span(0, AHEAD, near_tile, far_tile)
+    distance_span(0, AHEAD, near_tile, near_tile + 2)
     over = 1 + (row > 0).astype(jnp.int32) + (row < row_count - 1).astype(jnp.int32)
     across = 1 + (col > 0).astype(jnp.int32) + (col < col_count - 1).astype(jnp.int32)
     pl.semaphore_wait(barrier, over * across - 1)
     for (down, side), copy in zip(around, copies):
         pl.when(present(down, side))(copy.start)
+    distance_span(0, AHEAD, near_tile + 2, far_tile)
     distance_span(AHEAD, count // BATCH, near_tile, far_tile)
 
     for (down, side), copy in zip(around, copies):
@@ -400,7 +401,7 @@
     def weigh(piece, _):
         at = pl.ds(pl.multiple_of(piece * chunk, chunk), chunk)
         patch = jnp.dot(sums[at, :], band_ref[...], preferred_element_type=f32)
-        weights[at, :] = jnp.exp2(patch * EXPONENT)
+        weights[at, :] = jnp.exp2(patch)
         return 0
 
     def accumulate(turn, downs, sides, tile, _):

time: 51.6 us -> 51.7 us (level)
  the two profiles are of different devices: /device:TPU:1 before, /device:TPU:3 now
where the time goes in v10:
time: 51.7 us; the launch traced here: 51.6 us
  Pallas kernels  51.5 us (100%)
    pallas_call x1, Pallas kernels, filter_block(): pl.pallas_call(functools.partial(despeckle, sizes), out_shape=jax.ShapeDt...  49.3 us
    pallas_call x1, Pallas kernels, per_device(): pl.pallas_call(finish, out_shape=jax.ShapeDtypeStruct(coherency_field.sha...  2.2 us

profile of v10, /device:TPU:3, one launch (start us, length us, event | category | flops | bytes accessed | tf_op | source)
XLA Modules:
  0.0 51.6 jit_solution(150352970971175913)
XLA Ops:
  0.0 49.3 %shard_map.55.sums_ref = f32[10,64,256]{2,1,0:T(8,128)} custom-call(s32[2,120]{1,0:T(2,128)} %bitcast.1, f32[9,64,256]{2,1,0:T(8,128)} %field_ref.3, bf16[768,256]{1,0:T(8,128)(2,1)} %constant.6.clone.band_ref, bf16[384,256]{1,0:T(8,128)(2,1)} %constant.7.clone.pick_ref, bf16[13,16,128]{2,1,0:T(8,128)(2,1)} %constant.8.clone.keep_ref), custom_call_target="tpu_custom_call" | custom-call | tf_op jit(solution)/shard_map/pallas_call | solution.py:466
  49.4 2.2 %shard_map.56 = f32[9,64,256]{2,1,0:T(8,128)} custom-call(f32[9,64,256]{2,1,0:T(8,128)} %field_ref.3, f32[10,64,256]{2,1,0:T(8,128)} %shard_map.55.sums_ref), custom_call_target="tpu_custom_call" | custom-call | tf_op jit(solution)/shard_map/pallas_call | solution.py:507
